TPU v7x, 256 devices: a whole 4x4x8 slice. The times are simulated.
256 devices in a mesh: row: 16 (over y, z_hi), col: 16 (over z_lo, x, core).
Axes of the slice: x: 4, y: 4, z: 8 (z_hi: 4, z_lo: 2; z = z_hi * 2 + z_lo), core: 2. Of those that a mesh axis runs over, the one named last changes fastest.
Arguments:
- features: bfloat16 [256, 256, 384], P('row', 'col'), may hold values from -6 to 6
- norm_gain: float32 [384], replicated, may hold values from 0.5 to 1.5
- in_weight: bfloat16 [384, 1536], replicated, may hold values from -0.3125 to 0.3125
- conv_weight: float32 [3, 3, 768], replicated, may hold values from -2 to 2
- conv_bias: float32 [768], replicated, may hold values from -3 to 3
- proj_weight: bfloat16 [4, 768, 56], replicated, may hold values from -0.21875 to 0.21875
- step_weight: float32 [4, 24, 768], replicated, may hold values from -1.25 to 1.25
- step_bias: float32 [4, 768], replicated, may hold values from -9 to 2
- decay_log: float32 [4, 768, 16], replicated, may hold values from -3 to 0
- skip_gain: float32 [4, 768], replicated, may hold values from 0.02 to 0.2
- out_gain: float32 [768], replicated, may hold values from 0.5 to 1.5
- out_weight: bfloat16 [768, 384], replicated, may hold values from -0.21875 to 0.21875
Outputs:
- block_out: bfloat16 [256, 256, 384], P('row', 'col')
All inputs are finite; a program needn't handle non-finite values.
Results may differ from a plain program's by a relative error of at most 0.014.
Values may be sent and summed in bfloat16 or wider, within the bound.
A program may use at most 192 MiB of HBM per device.

v0:
```python
import functools

import jax
import jax.numpy as jnp
from jax import lax
from jax.experimental import pallas as pl
from jax.experimental.pallas import tpu as pltpu
from jax.sharding import PartitionSpec as P

F32 = jnp.float32
BF16 = jnp.bfloat16
MESH = pl.DeviceIdType.MESH
NT = (((1,), (1,)), ((), ()))
LANES = 128
LOG2E = 1.4426950408889634
VMEM = pl.BlockSpec(memory_space=pltpu.VMEM)


def dot(a, b):
    return jnp.dot(a, b, preferred_element_type=F32)


def dot_nt(a, b):
    return lax.dot_general(a, b, NT, preferred_element_type=F32)


def softplus(z):
    w = jnp.exp2(jnp.abs(z) * -LOG2E)
    small = w * (1.0 - w * (0.5 - w * (1.0 / 3.0)))
    return jnp.maximum(z, 0.0) + jnp.where(w < 0.01, small, jnp.log(1.0 + w))


def silu(v):
    return v / (1.0 + jnp.exp(-v))


def iota(shape, dim):
    return lax.broadcasted_iota(jnp.int32, shape, dim)


def cols(k):
    return slice(k * LANES, (k + 1) * LANES)


def place():
    return lax.axis_index("row"), lax.axis_index("col")


def greet(nr, nc, corners):
    row, col = place()
    sem = pltpu.get_barrier_semaphore()
    count = 0

    def signal(r, c):
        pl.semaphore_signal(sem, inc=1, device_id={"row": r, "col": c}, device_id_type=MESH)

    def along_col(k, _):
        signal(row, lax.rem(col + k, nc))
        return 0

    def along_row(k, _):
        signal(lax.rem(row + k, nr), col)
        return 0

    lax.fori_loop(1, nc, along_col, 0)
    lax.fori_loop(1, nr, along_row, 0)
    count = nc - 1 + nr - 1
    if corners:
        for dr in (1, nr - 1):
            for dc in (1, nc - 1):
                signal(lax.rem(row + dr, nr), lax.rem(col + dc, nc))
                count += 1
    return lambda: pl.semaphore_wait(sem, count)


def exchange(nr, nc, source, target, send_sem, recv_sem):
    row, col = place()

    def copy(axis, peer, owner, step):
        device = {"row": row, "col": peer} if axis == 0 else {"row": peer, "col": col}
        return pltpu.make_async_remote_copy(
            src_ref=source(axis, peer),
            dst_ref=target(axis, owner),
            send_sem=send_sem.at[axis, step],
            recv_sem=recv_sem.at[axis, owner],
            device_id=device,
            device_id_type=MESH,
        )

    def start(axis):
        me, count = ((col, nc), (row, nr))[axis]

        def one(step, _):
            copy(axis, lax.rem(me + step, count), me, step).start()
            return 0

        lax.fori_loop(1, count, one, 0)

    def wait(axis):
        me, count = ((col, nc), (row, nr))[axis]

        def one(step, _):
            peer = lax.rem(me + step, count)
            copy(axis, peer, me, step).wait_send()
            copy(axis, peer, peer, step).wait_recv()
            return 0

        lax.fori_loop(1, count, one, 0)

    return start, wait


def front_kernel(
    nr, nc, x_ref, gain_ref, wi_ref, cw_ref, cb_ref, gate_ref, lines_ref,
    nb_ref, nf_ref, strip_ref, halo_ref, pad_ref, act_ref, actt_ref, actf_ref, land_ref,
    hs_sem, hr_sem, send_sem, recv_sem,
):
    tr, tc, channels = x_ref.shape
    width = cb_ref.shape[1]
    tokens = tr * tc
    groups = width // LANES
    row, col = place()
    greeted = greet(nr, nc, True)

    step = 4 * tc

    def norm(i, _):
        v = x_ref[pl.ds(i * 4, 4)].reshape(step, channels).astype(F32)
        v = v - jnp.mean(v, axis=-1, keepdims=True)
        v = v * lax.rsqrt(jnp.mean(v * v, axis=-1, keepdims=True) + 1e-05) * gain_ref[...]
        at = pl.ds(pl.multiple_of(i * step, step), step)
        nb_ref[at, :] = v.astype(BF16)
        for k in range(channels // LANES):
            nf_ref[k, at, :] = v[:, cols(k)]
        return 0

    lax.fori_loop(0, tokens // step, norm, 0)
    for k in range(channels // LANES):
        strip_ref[0, :, cols(k)] = nf_ref[k, pl.ds(0, tr, stride=tc), :].astype(BF16)
        strip_ref[1, :, cols(k)] = nf_ref[k, pl.ds(tc - 1, tr, stride=tc), :].astype(BF16)
    top, bottom = nb_ref.at[pl.ds(0, tc)], nb_ref.at[pl.ds(tokens - tc, tc)]
    left, right = strip_ref.at[0], strip_ref.at[1]
    up, down = lax.rem(row + nr - 1, nr), lax.rem(row + 1, nr)
    west, east = lax.rem(col + nc - 1, nc), lax.rem(col + 1, nc)
    greeted()
    plan = (
        (bottom, down, col), (top, up, col), (right, row, east), (left, row, west),
        (bottom, down, east), (bottom, down, west), (top, up, east), (top, up, west),
    )
    halos = []
    for slot, (src, r, c) in enumerate(plan):
        halos.append(
            pltpu.make_async_remote_copy(
                src_ref=src, dst_ref=halo_ref.at[pl.ds(slot * tc, tc)],
                send_sem=hs_sem.at[slot], recv_sem=hr_sem.at[slot],
                device_id={"row": r, "col": c}, device_id_type=MESH,
            )
        )
        halos[-1].start()

    def project(i, _):
        at = pl.ds(pl.multiple_of(i * step, step), step)
        mixed = dot(nb_ref[at, :], wi_ref[...])
        gate_ref[at, :] = mixed[:, width:].astype(BF16)
        inner = mixed[:, :width].astype(BF16).astype(F32)
        for k in range(groups):
            pad_ref[k, pl.ds(1 + i * 4, 4), 8 : 8 + tc, :] = inner[:, cols(k)].reshape(4, tc, LANES)
        return 0

    lax.fori_loop(0, tokens // step, project, 0)
    for copy in halos:
        copy.wait()
    edge = dot(halo_ref[...], wi_ref[:, :width]).astype(BF16).astype(F32)
    north, south = row > 0, row < nr - 1
    lwest, least = col > 0, col < nc - 1

    def seen(slot, ok, first=0, count=None):
        part = edge[slot * tc + first : slot * tc + first + (tc if count is None else count)]
        return jnp.where(ok, part, 0.0)

    n_all, s_all = seen(0, north), seen(1, south)
    w_all, e_all = seen(2, lwest), seen(3, least)
    nw, ne = seen(4, north & lwest, tc - 8, 8), seen(5, north & least, 0, 8)
    sw, se = seen(6, south & lwest, tc - 8, 8), seen(7, south & least, 0, 8)
    for k in range(groups):
        pad_ref[k, 0, 8 : 8 + tc, :] = n_all[:, cols(k)]
        pad_ref[k, tr + 1, 8 : 8 + tc, :] = s_all[:, cols(k)]
        pad_ref[k, 0, 0:8, :] = nw[:, cols(k)]
        pad_ref[k, 0, 8 + tc : 16 + tc, :] = ne[:, cols(k)]
        pad_ref[k, tr + 1, 0:8, :] = sw[:, cols(k)]
        pad_ref[k, tr + 1, 8 + tc : 16 + tc, :] = se[:, cols(k)]
        for r in range(tr):
            pad_ref[k, 1 + r, 7:8, :] = w_all[r : r + 1, cols(k)]
            pad_ref[k, 1 + r, 8 + tc : 9 + tc, :] = e_all[r : r + 1, cols(k)]

    def convolve(r, _):
        for k in range(groups):
            total = jnp.broadcast_to(cb_ref[:, cols(k)], (tc, LANES))
            for a in range(3):
                for b in range(3):
                    total = total + pad_ref[k, r + a, 7 + b : 7 + b + tc, :] * cw_ref[a, b : b + 1, cols(k)]
            done = silu(total).astype(BF16)
            act_ref[r, :, cols(k)] = done
            actf_ref[k, pl.ds(pl.multiple_of(r * tc, tc), tc), :] = done.astype(F32)
        return 0

    lax.fori_loop(0, tr, convolve, 0)

    def source(axis, peer):
        return act_ref.at[peer] if axis == 0 else actt_ref.at[peer]

    def target(axis, owner):
        return land_ref.at[axis, pl.ds(pl.multiple_of(owner * tc, tc), tc)]

    start, wait = exchange(nr, nc, source, target, send_sem, recv_sem)
    start(0)

    def flip(j, _):
        for k in range(groups):
            actt_ref[j, :, cols(k)] = actf_ref[k, pl.ds(j, tr, stride=tc), :].astype(BF16)
        return 0

    lax.fori_loop(0, tc, flip, 0)
    start(1)
    land_ref[0, pl.ds(pl.multiple_of(col * tc, tc), tc), :] = act_ref[col]
    land_ref[1, pl.ds(pl.multiple_of(row * tr, tr), tr), :] = actt_ref[row]
    wait(0)
    wait(1)
    lines_ref[...] = land_ref[...]


def scan_kernel(
    chunk, u_ref, pw_ref, sw_ref, sb_ref, dl_ref, sk_ref, y_ref,
    ph_ref, pl_ref, s_ref, du_ref, bb_ref, mc_ref, dec_ref, ha_ref, hb_ref, acc_ref,
):
    length, width = u_ref.shape
    rank = sw_ref.shape[1]
    states = dl_ref.shape[1]
    parts = pw_ref.shape[1]
    span = 16
    line = pl.program_id(0)
    held = (ha_ref, hb_ref)
    kk, cc = iota((parts, span * states), 0), iota((parts, span * states), 1)
    repeat = (kk == rank + states + lax.rem(cc, states)).astype(BF16)
    mask = lax.rem(iota((length, span * states), 0), span) == iota((length, span * states), 1) // states
    ones = jnp.ones((LANES, LANES), BF16)
    lane = iota((states, LANES), 1)

    def prepare(d, _):
        p = dot_nt(u_ref[...], pw_ref[d])
        high = p.astype(BF16)
        ph_ref[d] = high
        pl_ref[d] = (p - high.astype(F32)).astype(BF16)
        mc_ref[d] = jnp.where(mask, dot(high, repeat), 0.0).astype(BF16)
        enter = dot_nt(pw_ref[d, rank : rank + states, :], u_ref[...])
        for h in range(length // LANES):
            for g in range(0, LANES, span):
                spread = [jnp.where(lane == g + i, enter[:, cols(h)], 0.0) for i in range(span)]
                at = (h * LANES + g) * states
                bb_ref[d, at : at + span * states, :] = dot(jnp.concatenate(spread, axis=0).astype(BF16), ones)
        dec_ref[d] = jnp.exp(dl_ref[d]) * -LOG2E
        sw = sw_ref[d]
        swh = sw.astype(BF16)
        swl = (sw - swh.astype(F32)).astype(BF16)
        bias = sb_ref[pl.ds(line * 2 + d, 1), :]

        def step_size(i, _):
            at = pl.ds(pl.multiple_of(i * 32, 32), 32)
            a = ph_ref[d, at, :rank]
            s = softplus(dot(a, swh) + (dot(a, swl) + dot(pl_ref[d, at, :rank], swh)) + bias)
            du = s * u_ref[at, :].astype(F32)
            for k in range(width // LANES):
                s_ref[d, k, at, :] = s[:, cols(k)]
                du_ref[d, k, at, :] = du[:, cols(k)]
            return 0

        lax.fori_loop(0, length // 32, step_size, 0)
        return 0

    lax.fori_loop(0, 2, prepare, 0)
    skip = sk_ref[pl.ds(line * 2, 1), :] + sk_ref[pl.ds(line * 2 + 1, 1), :]

    def begin(i, _):
        at = pl.ds(pl.multiple_of(i * 32, 32), 32)
        acc_ref[at, :] = u_ref[at, :].astype(F32) * skip
        return 0

    lax.fori_loop(0, length // 32, begin, 0)
    blocks = length // span
    per = chunk // LANES

    for g0 in range(0, width // LANES, per):
        c0 = g0 * LANES
        dec = [[[dec_ref[d, 8 * v : 8 * v + 8, cols(g0 + k)] for v in range(2)] for k in range(per)] for d in range(2)]

        def leave(slot, i, d):
            b = pl.multiple_of((i if d == 0 else blocks - 1 - i) * span, span)
            states_now = jnp.concatenate([held[slot][d, k] for k in range(per)], axis=1)
            acc_ref[pl.ds(b, span), c0 : c0 + chunk] += dot(mc_ref[d, pl.ds(b, span), :], states_now)

        def advance(slot, i, h):
            base = (i * span, (blocks - 1 - i) * span)
            for j in range(span):
                for d in range(2):
                    jj = j if d == 0 else span - 1 - j
                    t = base[d] + jj
                    enter = [bb_ref[d, pl.ds(pl.multiple_of(t * states + 8 * v, 8), 8), :] for v in range(2)]
                    for k in range(per):
                        s = s_ref[d, g0 + k, pl.ds(t, 8, stride=0), :]
                        du = du_ref[d, g0 + k, pl.ds(t, 8, stride=0), :]
                        now = [jnp.exp2(s * dec[d][k][v]) * h[d][k][v] + du * enter[v] for v in range(2)]
                        h[d][k] = now
                        held[slot][d, k, jj * states : (jj + 1) * states, :] = jnp.concatenate(now, axis=0).astype(BF16)
            return h

        def body(i, h):
            h = [[list(v) for v in part] for part in h]
            for d in range(2):
                leave(1, jnp.maximum(2 * i - 1, 0), d)
            h = advance(0, 2 * i, h)
            for d in range(2):
                leave(0, 2 * i, d)
            h = advance(1, 2 * i + 1, h)
            return tuple(tuple(tuple(v) for v in part) for part in h)

        hb_ref[...] = jnp.zeros_like(hb_ref)
        zero = jnp.zeros((8, LANES), F32)
        lax.fori_loop(0, blocks // 2, body, tuple(tuple((zero, zero) for _ in range(per)) for _ in range(2)))
        for d in range(2):
            leave(1, blocks - 1, d)
    y_ref[...] = acc_ref[...].astype(BF16)


def back_kernel(
    nr, nc, y_ref, gate_ref, gain_ref, wo_ref, out_ref, land_ref, cf_ref, go_ref, send_sem, recv_sem,
):
    tr, tc, _ = out_ref.shape
    width = wo_ref.shape[0]
    groups = width // LANES
    row, col = place()
    greet(nr, nc, False)()

    def source(axis, peer):
        return y_ref.at[axis, pl.ds(pl.multiple_of(peer * tc, tc), tc)]

    def target(axis, owner):
        return land_ref.at[axis, owner]

    start, wait = exchange(nr, nc, source, target, send_sem, recv_sem)
    start(0)
    start(1)
    land_ref[0, col] = y_ref[0, pl.ds(pl.multiple_of(col * tc, tc), tc), :]
    land_ref[1, row] = y_ref[1, pl.ds(pl.multiple_of(row * tr, tr), tr), :]
    wait(0)
    wait(1)

    def widen(j, _):
        for k in range(groups):
            cf_ref[k, pl.ds(pl.multiple_of(j * tr, tr), tr), :] = land_ref[1, j, :, cols(k)].astype(F32)
        return 0

    lax.fori_loop(0, tc, widen, 0)

    def finish(r, _):
        other = jnp.concatenate([cf_ref[k, pl.ds(r, tc, stride=tr), :] for k in range(groups)], axis=1)
        v = land_ref[0, r].astype(F32) + other
        v = v - jnp.mean(v, axis=-1, keepdims=True)
        v = v * lax.rsqrt(jnp.mean(v * v, axis=-1, keepdims=True) + 1e-05) * gain_ref[...]
        at = pl.ds(pl.multiple_of(r * tc, tc), tc)
        go_ref[at, :] = (v * silu(gate_ref[at, :].astype(F32))).astype(BF16)
        return 0

    lax.fori_loop(0, tr, finish, 0)
    out_ref[...] = dot(go_ref[...], wo_ref[...]).astype(BF16).reshape(out_ref.shape)


def local(
    nr, nc, features, norm_gain, in_weight, conv_weight, conv_bias, proj_weight, step_weight, step_bias,
    decay_log, skip_gain, out_gain, out_weight,
):
    tr, tc, channels = features.shape
    width = out_weight.shape[0]
    tokens = tr * tc
    groups = width // LANES
    length = tc * nc
    dma = pltpu.SemaphoreType.DMA
    gate, lines = pl.pallas_call(
        functools.partial(front_kernel, nr, nc),
        out_shape=(
            jax.ShapeDtypeStruct((tokens, width), BF16),
            jax.ShapeDtypeStruct((2, length, width), BF16),
        ),
        in_specs=[VMEM] * 5,
        out_specs=(VMEM, VMEM),
        scratch_shapes=[
            pltpu.VMEM((tokens, channels), BF16),
            pltpu.VMEM((channels // LANES, tokens, LANES), F32),
            pltpu.VMEM((2, tr, channels), BF16),
            pltpu.VMEM((8 * tc, channels), BF16),
            pltpu.VMEM((groups, tr + 2, tc + 16, LANES), F32),
            pltpu.VMEM((tr, tc, width), BF16),
            pltpu.VMEM((tc, tr, width), BF16),
            pltpu.VMEM((groups, tokens, LANES), F32),
            pltpu.VMEM((2, length, width), BF16),
            dma((8,)), dma((8,)), dma((2, nc)), dma((2, nc)),
        ],
        compiler_params=pltpu.CompilerParams(collective_id=0, has_side_effects=True, vmem_limit_bytes=40 << 20),
    )(features, norm_gain[None], in_weight, conv_weight, conv_bias[None])

    pw = jnp.swapaxes(proj_weight, 1, 2)
    dl = jnp.swapaxes(decay_log, 1, 2)
    rank, states = step_weight.shape[1], dl.shape[1]
    span, chunk = 16, 256
    pair = lambda a: pl.BlockSpec((2,) + a.shape[1:], lambda i: (i,) + (0,) * (a.ndim - 1))
    whole = lambda a: pl.BlockSpec(a.shape, lambda i: (0,) * a.ndim)
    y = pl.pallas_call(
        functools.partial(scan_kernel, chunk),
        out_shape=jax.ShapeDtypeStruct((2, length, width), BF16),
        grid=(2,),
        in_specs=[
            pl.BlockSpec((None, length, width), lambda i: (i, 0, 0)),
            pair(pw), pair(step_weight), whole(step_bias), pair(dl), whole(skip_gain),
        ],
        out_specs=pl.BlockSpec((None, length, width), lambda i: (i, 0, 0)),
        scratch_shapes=[
            pltpu.VMEM((2, length, pw.shape[1]), BF16),
            pltpu.VMEM((2, length, pw.shape[1]), BF16),
            pltpu.VMEM((2, groups, length, LANES), F32),
            pltpu.VMEM((2, groups, length, LANES), F32),
            pltpu.VMEM((2, length * states, LANES), F32),
            pltpu.VMEM((2, length, span * states), BF16),
            pltpu.VMEM((2, states, width), F32),
            pltpu.VMEM((2, chunk // LANES, span * states, LANES), BF16),
            pltpu.VMEM((2, chunk // LANES, span * states, LANES), BF16),
            pltpu.VMEM((length, width), F32),
        ],
        compiler_params=pltpu.CompilerParams(vmem_limit_bytes=48 << 20),
    )(lines, pw, step_weight, step_bias, dl, skip_gain)

    return pl.pallas_call(
        functools.partial(back_kernel, nr, nc),
        out_shape=jax.ShapeDtypeStruct(features.shape, BF16),
        in_specs=[VMEM] * 4,
        out_specs=VMEM,
        scratch_shapes=[
            pltpu.VMEM((2, tc, tr, width), BF16),
            pltpu.VMEM((groups, tokens, LANES), F32),
            pltpu.VMEM((tokens, width), BF16),
            dma((2, nc)), dma((2, nc)),
        ],
        compiler_params=pltpu.CompilerParams(collective_id=1, has_side_effects=True, vmem_limit_bytes=40 << 20),
    )(y, gate, out_gain[None], out_weight)


def solution(mesh):
    nr, nc = mesh.shape["row"], mesh.shape["col"]
    in_specs = (P("row", "col", None), P(), P(), P(), P(), P(), P(), P(), P(), P(), P(), P())
    return jax.shard_map(
        functools.partial(local, nr, nc), mesh=mesh, in_specs=in_specs, out_specs=P("row", "col", None), check_vma=False
    )
```

profile of v0, /device:TPU:1, one launch (start us, length us, event | category | flops | bytes accessed | tf_op | source)
XLA Modules:
  0.0 93.9 jit_solution(18240037125476477022)
XLA Ops:
  0.0 0.7 broadcast_in_dim.10.cb_ref
  0.7 0.7 broadcast_in_dim.9.gain_ref
  1.4 0.0 copy-start
  1.4 1.3 %copy-done = bf16[384,1536]{1,0:T(8,128)(2,1)S(1)} copy-done((bf16[384,1536]{1,0:T(8,128)(2,1)S(1)}, bf16[384,1536]{1,0:T(8,128)(2,1)}, u32[]{:S(2)}) %copy-start) | copy-done | bytes 1179672
  2.6 0.0 copy-start.4
  2.6 0.9 copy-done.4
  3.6 0.0 copy-start.6
  3.6 0.8 copy-done.6
  4.3 0.0 copy-start.2
  4.3 0.0 copy-start.3
  4.3 0.0 copy-start.5
  4.3 0.0 copy-start.7
  4.4 0.0 copy-start.8
  4.4 34.7 %shard_map.118 = (bf16[256,768]{1,0:T(8,128)(2,1)S(1)}, bf16[2,256,768]{2,1,0:T(8,128)(2,1)S(1)}) custom-call(bf16[16,16,384]{2,1,0:T(8,128)(2,1)S(1)} %copy-done.4, f32[1,384]{1,0:T(1,128)S(1)} %broadcast_in_dim.9.gain_ref, bf16[384,1536]{1,0:T(8,128)(2,1)S(1)} %copy-done, f32[3,3,768]{2,1,0:T(4,128)S(1)} %copy-done.6, f32[1,768]{1,0:T(1,128)S(1)} %broadcast_in_dim.10.cb_ref), custom_call_target="tpu_custom_call" | custom-call | tf_op jit(solution)/shard_map/pallas_call | solution.py:387
  39.1 0.0 copy-done.2
  39.1 0.0 copy-done.3
  39.1 0.0 copy-done.5
  39.1 0.0 copy-done.7
  39.1 0.0 copy-done.8
  39.1 0.0 copy-start.9
  39.1 0.0 copy-start.1
  39.1 30.6 %shard_map.119.y_ref = bf16[2,256,768]{2,1,0:T(8,128)(2,1)S(1)} custom-call(bf16[2,256,768]{2,1,0:T(8,128)(2,1)S(1)} %get-tuple-element.7.u_ref, bf16[4,56,768]{2,1,0:T(8,128)(2,1)S(1)} %bitcast.2, f32[4,24,768]{2,1,0:T(8,128)S(1)} %copy-done.3, f32[4,768]{1,0:T(4,128)S(1)} %copy-done.7, f32[4,16,768]{2,1,0:T(8,128)S(1)} %bitcast.3, f32[4,768]{1,0:T(4,128)S(1)} %copy-done.8), custom_call_target="tpu_custom_call" | custom-call | tf_op jit(solution)/shard_map/pallas_call | solution.py:416
  69.7 0.0 copy-done.9
  69.7 0.0 copy-done.1
  69.7 23.5 %shard_map.120 = bf16[16,16,384]{2,1,0:T(8,128)(2,1)S(1)} custom-call(bf16[2,256,768]{2,1,0:T(8,128)(2,1)S(1)} %shard_map.119.y_ref, bf16[256,768]{1,0:T(8,128)(2,1)S(1)} %get-tuple-element.8.gate_ref, f32[1,768]{1,0:T(1,128)S(1)} %broadcast_in_dim.11.gain_ref, bf16[768,384]{1,0:T(8,128)(2,1)S(1)} %copy-done.1), custom_call_target="tpu_custom_call" | custom-call | tf_op jit(solution)/shard_map/pallas_call | solution.py:440
  93.2 0.7 copy.14
  (1 shorter events, 0.0 us)
Async XLA Ops:
  1.4 1.3 %copy-start = (bf16[384,1536]{1,0:T(8,128)(2,1)S(1)}, bf16[384,1536]{1,0:T(8,128)(2,1)}, u32[]{:S(2)}) copy-start(bf16[384,1536]{1,0:T(8,128)(2,1)} %wi_ref.1) | copy-start | bytes 3538948
  2.6 0.9 copy-start.4
  3.6 0.8 copy-start.6
  4.3 34.7 %copy-start.2 = (bf16[4,768,56]{1,2,0:T(8,128)(2,1)S(1)}, bf16[4,768,56]{1,2,0:T(8,128)(2,1)}, u32[]{:S(2)}) copy-start(bf16[4,768,56]{1,2,0:T(8,128)(2,1)} %param.17) | copy-start | bytes 1032196
  4.3 34.7 %copy-start.3 = (f32[4,24,768]{2,1,0:T(8,128)S(1)}, f32[4,24,768]{2,1,0:T(8,128)}, u32[]{:S(2)}) copy-start(f32[4,24,768]{2,1,0:T(8,128)} %sw_ref.1) | copy-start | bytes 884740
  4.3 34.8 %copy-start.5 = (f32[4,768,16]{1,2,0:T(8,128)S(1)}, f32[4,768,16]{1,2,0:T(8,128)}, u32[]{:S(2)}) copy-start(f32[4,768,16]{1,2,0:T(8,128)} %param.20) | copy-start | bytes 589828
  4.3 34.8 %copy-start.7 = (f32[4,768]{1,0:T(4,128)S(1)}, f32[4,768]{1,0:T(4,128)}, u32[]{:S(2)}) copy-start(f32[4,768]{1,0:T(4,128)} %sb_ref.1) | copy-start | bytes 36868
  4.4 34.8 %copy-start.8 = (f32[4,768]{1,0:T(4,128)S(1)}, f32[4,768]{1,0:T(4,128)}, u32[]{:S(2)}) copy-start(f32[4,768]{1,0:T(4,128)} %sk_ref.1) | copy-start | bytes 36868
  39.1 30.6 %copy-start.9 = (f32[768]{0:T(1024)S(1)}, f32[768]{0:T(1024)}, u32[]{:S(2)}) copy-start(f32[768]{0:T(1024)} %param.22) | copy-start | bytes 9220
  39.1 30.6 %copy-start.1 = (bf16[768,384]{1,0:T(8,128)(2,1)S(1)}, bf16[768,384]{1,0:T(8,128)(2,1)}, u32[]{:S(2)}) copy-start(bf16[768,384]{1,0:T(8,128)(2,1)} %wo_ref.1) | copy-start | bytes 1769476
where the time goes:
time: 94.2 us; the launch traced here: 93.9 us
  Pallas kernels  88.8 us (94%)
  local copies, waits for them, and re-layouts  5.05 us (5%)
    pallas_call x1, Pallas kernels, local(): pl.pallas_call(functools.partial(front_kernel, nr, nc), out_shape=(jax.Sh...  34.7 us
    pallas_call x1, Pallas kernels, local(): pl.pallas_call(functools.partial(scan_kernel, chunk), out_shape=jax.Shape...  30.6 us
    pallas_call x1, Pallas kernels, local(): pl.pallas_call(functools.partial(back_kernel, nr, nc), out_shape=jax.Shap...  23.5 us
    unnamed x21, local copies, waits for them, and re-layouts  3.68 us

commit v1 on v0

v1 whole, which is shorter than its diff:
```python
import functools

import jax
import jax.numpy as jnp
from jax import lax
from jax.experimental import pallas as pl
from jax.experimental.pallas import tpu as pltpu
from jax.sharding import PartitionSpec as P

F32 = jnp.float32
BF16 = jnp.bfloat16
MESH = pl.DeviceIdType.MESH
NT = (((1,), (1,)), ((), ()))
LANES = 128
LOG2E = 1.4426950408889634
VMEM = pl.BlockSpec(memory_space=pltpu.VMEM)


def dot(a, b):
    return jnp.dot(a, b, preferred_element_type=F32)


def dot_nt(a, b):
    return lax.dot_general(a, b, NT, preferred_element_type=F32)


def softplus(z):
    w = jnp.exp2(jnp.abs(z) * -LOG2E)
    small = w * (1.0 - w * (0.5 - w * (1.0 / 3.0)))
    return jnp.maximum(z, 0.0) + jnp.where(w < 0.01, small, jnp.log(1.0 + w))


def silu(v):
    return v / (1.0 + jnp.exp(-v))


def iota(shape, dim):
    return lax.broadcasted_iota(jnp.int32, shape, dim)


def cols(k):
    return slice(k * LANES, (k + 1) * LANES)


def place():
    return lax.axis_index("row"), lax.axis_index("col")


def greet(nr, nc):
    row, col = place()
    sem = pltpu.get_barrier_semaphore()

    def signal(r, c):
        pl.semaphore_signal(sem, inc=1, device_id={"row": r, "col": c}, device_id_type=MESH)

    def along_col(k, _):
        signal(row, lax.rem(col + k, nc))
        return 0

    def along_row(k, _):
        signal(lax.rem(row + k, nr), col)
        return 0

    lax.fori_loop(1, nc, along_col, 0)
    lax.fori_loop(1, nr, along_row, 0)
    for dr in (1, nr - 1):
        for dc in (1, nc - 1):
            signal(lax.rem(row + dr, nr), lax.rem(col + dc, nc))
    return lambda: pl.semaphore_wait(sem, nr + nc + 2)


def remote(src, dst, send_sem, recv_sem, r, c):
    return pltpu.make_async_remote_copy(
        src_ref=src, dst_ref=dst, send_sem=send_sem, recv_sem=recv_sem,
        device_id={"row": r, "col": c}, device_id_type=MESH,
    )


def block_kernel(
    n, per, x_hbm, gain_ref, wi_hbm, cw_ref, cb_ref, pw_hbm, sw_hbm, sb_ref, dl_hbm, sk_ref, og_ref, wo_hbm, out_ref,
    x_ref, wi_ref, pw_ref, sw_ref, dl_ref, wo_ref,
    nb_ref, nf_ref, strip_ref, halo_ref, pad_ref, act_ref, actt_ref, actf_ref, line_ref, gate_ref,
    ph_ref, pl_ref, s_ref, du_ref, bb_ref, mc_ref, dec_ref, ha_ref, hb_ref, acc_ref, y_ref, land_ref, cf_ref, go_ref,
    own_sem, hs_sem, hr_sem, ts_sem, tr_sem, ys_sem, yr_sem,
):
    tr, tc, channels = x_ref.shape
    width = cb_ref.shape[-1]
    tokens = tr * tc
    groups = width // LANES
    chunks = groups // per
    chunk = per * LANES
    length = line_ref.shape[1]
    rank, states, parts = sw_ref.shape[1], dl_ref.shape[1], pw_ref.shape[1]
    row, col = place()
    fetch = [
        pltpu.make_async_copy(src, dst, own_sem.at[i])
        for i, (src, dst) in enumerate(
            ((x_hbm, x_ref), (wi_hbm, wi_ref), (pw_hbm, pw_ref), (sw_hbm, sw_ref), (dl_hbm, dl_ref), (wo_hbm, wo_ref))
        )
    ]
    for copy in fetch:
        copy.start()
    greeted = greet(n, n)

    def mine(axis):
        return col + axis * (row - col)

    def across(axis, peer):
        return row + axis * (peer - row), peer + axis * (col - peer)

    def every(axis, one):
        me = mine(axis)

        def body(step, _):
            one(step, lax.rem(me + step, n))
            return 0

        lax.fori_loop(1, n, body, 0)

    def tile(i):
        return pl.ds(pl.multiple_of(i * tc, tc), tc)

    step = 4 * tc
    fetch[0].wait()

    def norm(i, _):
        v = x_ref[pl.ds(i * 4, 4)].reshape(step, channels).astype(F32)
        v = v - jnp.mean(v, axis=-1, keepdims=True)
        v = v * lax.rsqrt(jnp.mean(v * v, axis=-1, keepdims=True) + 1e-05) * gain_ref[...].reshape(1, channels)
        at = pl.ds(pl.multiple_of(i * step, step), step)
        nb_ref[at, :] = v.astype(BF16)
        for k in range(channels // LANES):
            nf_ref[k, at, :] = v[:, cols(k)]
        return 0

    lax.fori_loop(0, tokens // step, norm, 0)
    for k in range(channels // LANES):
        strip_ref[0, :, cols(k)] = nf_ref[k, pl.ds(0, tr, stride=tc), :].astype(BF16)
        strip_ref[1, :, cols(k)] = nf_ref[k, pl.ds(tc - 1, tr, stride=tc), :].astype(BF16)
    top, bottom = nb_ref.at[pl.ds(0, tc)], nb_ref.at[pl.ds(tokens - tc, tc)]
    left, right = strip_ref.at[0], strip_ref.at[1]
    up, down = lax.rem(row + n - 1, n), lax.rem(row + 1, n)
    west, east = lax.rem(col + n - 1, n), lax.rem(col + 1, n)
    greeted()
    plan = (
        (bottom, down, col), (top, up, col), (right, row, east), (left, row, west),
        (bottom, down, east), (bottom, down, west), (top, up, east), (top, up, west),
    )
    halos = [
        remote(src, halo_ref.at[pl.ds(slot * tc, tc)], hs_sem.at[slot], hr_sem.at[slot], r, c)
        for slot, (src, r, c) in enumerate(plan)
    ]
    for copy in halos:
        copy.start()
    fetch[1].wait()

    def project(i, _):
        at = pl.ds(pl.multiple_of(i * step, step), step)
        inner = dot(nb_ref[at, :], wi_ref[:, :width]).astype(BF16).astype(F32)
        for k in range(groups):
            pad_ref[k, pl.ds(1 + i * 4, 4), 8 : 8 + tc, :] = inner[:, cols(k)].reshape(4, tc, LANES)
        return 0

    lax.fori_loop(0, tokens // step, project, 0)
    for copy in halos:
        copy.wait()
    edge = dot(halo_ref[...], wi_ref[:, :width]).astype(BF16).astype(F32)
    north, south = row > 0, row < n - 1
    lwest, least = col > 0, col < n - 1

    def seen(slot, ok, first=0, count=tc):
        return jnp.where(ok, edge[slot * tc + first : slot * tc + first + count], 0.0)

    n_all, s_all = seen(0, north), seen(1, south)
    w_all, e_all = seen(2, lwest), seen(3, least)
    nw, ne = seen(4, north & lwest, tc - 8, 8), seen(5, north & least, 0, 8)
    sw, se = seen(6, south & lwest, tc - 8, 8), seen(7, south & least, 0, 8)
    for k in range(groups):
        pad_ref[k, 0, 8 : 8 + tc, :] = n_all[:, cols(k)]
        pad_ref[k, tr + 1, 8 : 8 + tc, :] = s_all[:, cols(k)]
        pad_ref[k, 0, 0:8, :] = nw[:, cols(k)]
        pad_ref[k, 0, 8 + tc : 16 + tc, :] = ne[:, cols(k)]
        pad_ref[k, tr + 1, 0:8, :] = sw[:, cols(k)]
        pad_ref[k, tr + 1, 8 + tc : 16 + tc, :] = se[:, cols(k)]
        for r in range(tr):
            pad_ref[k, 1 + r, 7:8, :] = w_all[r : r + 1, cols(k)]
            pad_ref[k, 1 + r, 8 + tc : 9 + tc, :] = e_all[r : r + 1, cols(k)]
    bias = cb_ref[...].reshape(1, width)

    def convolve(r, _):
        for k in range(groups):
            total = jnp.broadcast_to(bias[:, cols(k)], (tc, LANES))
            for a in range(3):
                for b in range(3):
                    total = total + pad_ref[k, r + a, 7 + b : 7 + b + tc, :] * cw_ref[a, b : b + 1, cols(k)]
            done = silu(total).astype(BF16)
            act_ref[r, :, cols(k)] = done
            actf_ref[k, tile(r), :] = done.astype(F32)
        return 0

    lax.fori_loop(0, tr, convolve, 0)

    def token_copy(axis, step, peer, owner):
        src = (act_ref if axis == 0 else actt_ref).at[peer]
        return remote(
            src, line_ref.at[axis, tile(owner)], ts_sem.at[axis, step], tr_sem.at[axis, owner], *across(axis, peer)
        )

    def token_arrival(axis, step, peer):
        remote(
            act_ref.at[0], line_ref.at[axis, tile(peer)], ts_sem.at[axis, step], tr_sem.at[axis, peer],
            *across(axis, peer),
        ).wait_recv()

    every(0, lambda step, peer: token_copy(0, step, peer, col).start())

    def flip(j, _):
        for k in range(groups):
            actt_ref[j, :, cols(k)] = actf_ref[k, pl.ds(j, tr, stride=tc), :].astype(BF16)
        return 0

    lax.fori_loop(0, tc, flip, 0)
    every(1, lambda step, peer: token_copy(1, step, peer, row).start())
    line_ref[0, tile(col), :] = act_ref[col]
    line_ref[1, tile(row), :] = actt_ref[row]

    def gates(i, _):
        at = pl.ds(pl.multiple_of(i * step, step), step)
        gate = dot(nb_ref[at, :], wi_ref[:, width:]).astype(BF16).astype(F32)
        gate_ref[at, :] = silu(gate)
        return 0

    lax.fori_loop(0, tokens // step, gates, 0)
    fetch[4].wait()

    def rates(d, _):
        for k in range(groups):
            dec_ref[d, k] = jnp.exp(dl_ref[d, :, cols(k)]) * -LOG2E
        return 0

    lax.fori_loop(0, dl_ref.shape[0], rates, 0)
    for i in (2, 3, 5):
        fetch[i].wait()

    span = 16
    blocks = length // span
    held = (ha_ref, hb_ref)
    kk, cc = iota((parts, span * states), 0), iota((parts, span * states), 1)
    lane = iota((states, LANES), 1)

    def scan_line(line, _):
        every(line, lambda step, peer: token_arrival(line, step, peer))

        def prepare(d, _):
            which = line * 2 + d
            repeat = (kk == rank + states + lax.rem(cc, states)).astype(BF16)
            mask = lax.rem(iota((length, span * states), 0), span) == iota((length, span * states), 1) // states
            u = line_ref[line]
            p = dot_nt(u, pw_ref[which])
            high = p.astype(BF16)
            ph_ref[d] = high
            pl_ref[d] = (p - high.astype(F32)).astype(BF16)
            mc_ref[d] = jnp.where(mask, dot(high, repeat), 0.0).astype(BF16)
            enter = dot_nt(pw_ref[which, rank : rank + states, :], u)
            ones = jnp.ones((LANES, LANES), BF16)
            for h in range(length // LANES):
                for g in range(0, LANES, span):
                    spread = [jnp.where(lane == g + i, enter[:, cols(h)], 0.0) for i in range(span)]
                    at = (h * LANES + g) * states
                    bb_ref[d, at : at + span * states, :] = dot(jnp.concatenate(spread, axis=0).astype(BF16), ones)
            weight = sw_ref[which]
            swh = weight.astype(BF16)
            swl = (weight - swh.astype(F32)).astype(BF16)
            shift = sb_ref[pl.ds(which, 1), :]

            def step_size(i, _):
                at = pl.ds(pl.multiple_of(i * 32, 32), 32)
                a = ph_ref[d, at, :rank]
                s = softplus(dot(a, swh) + (dot(a, swl) + dot(pl_ref[d, at, :rank], swh)) + shift)
                du = s * line_ref[line, at, :].astype(F32)
                for k in range(groups):
                    s_ref[d, k, at, :] = s[:, cols(k)]
                    du_ref[d, k, at, :] = du[:, cols(k)]
                return 0

            lax.fori_loop(0, length // 32, step_size, 0)
            return 0

        lax.fori_loop(0, 2, prepare, 0)
        skip = sk_ref[pl.ds(line * 2, 1), :] + sk_ref[pl.ds(line * 2 + 1, 1), :]

        def begin(i, _):
            at = pl.ds(pl.multiple_of(i * 32, 32), 32)
            v = line_ref[line, at, :].astype(F32) * skip
            for c in range(chunks):
                acc_ref[c, at, :] = v[:, c * chunk : (c + 1) * chunk]
            return 0

        lax.fori_loop(0, length // 32, begin, 0)

        def scan_chunk(c, _):
            g0 = c * per
            dec = [
                [[dec_ref[line * 2 + d, g0 + k, 8 * v : 8 * v + 8, :] for v in range(2)] for k in range(per)]
                for d in range(2)
            ]

            def leave(slot, i, d):
                b = pl.multiple_of((i if d == 0 else blocks - 1 - i) * span, span)
                states_now = jnp.concatenate([held[slot][d, k] for k in range(per)], axis=1)
                acc_ref[c, pl.ds(b, span), :] += dot(mc_ref[d, pl.ds(b, span), :], states_now)

            def advance(slot, i, h):
                base = (i * span, (blocks - 1 - i) * span)
                for j in range(span):
                    for d in range(2):
                        jj = j if d == 0 else span - 1 - j
                        t = base[d] + jj
                        enter = [bb_ref[d, pl.ds(pl.multiple_of(t * states + 8 * v, 8), 8), :] for v in range(2)]
                        for k in range(per):
                            s = s_ref[d, g0 + k, pl.ds(t, 8, stride=0), :]
                            du = du_ref[d, g0 + k, pl.ds(t, 8, stride=0), :]
                            now = [jnp.exp2(s * dec[d][k][v]) * h[d][k][v] + du * enter[v] for v in range(2)]
                            h[d][k] = now
                            held[slot][d, k, jj * states : (jj + 1) * states, :] = jnp.concatenate(
                                now, axis=0
                            ).astype(BF16)
                return h

            def body(i, h):
                h = [[list(v) for v in part] for part in h]
                for d in range(2):
                    leave(1, jnp.maximum(2 * i - 1, 0), d)
                h = advance(0, 2 * i, h)
                for d in range(2):
                    leave(0, 2 * i, d)
                h = advance(1, 2 * i + 1, h)
                return tuple(tuple(tuple(v) for v in part) for part in h)

            hb_ref[...] = jnp.zeros_like(hb_ref)
            zero = jnp.zeros((8, LANES), F32)
            lax.fori_loop(0, blocks // 2, body, tuple(tuple((zero, zero) for _ in range(per)) for _ in range(2)))
            for d in range(2):
                leave(1, blocks - 1, d)
            y_ref[line, c] = acc_ref[c].astype(BF16)
            me = mine(line)
            every(line, lambda step, peer: result_copy(line, c, step, peer, me).start())
            land_ref[line, c, me] = y_ref[line, c, tile(me), :]
            return 0

        lax.fori_loop(0, chunks, scan_chunk, 0)
        return 0

    def result_copy(axis, c, step, peer, owner):
        return remote(
            y_ref.at[axis, c, tile(peer)], land_ref.at[axis, c, owner], ys_sem.at[axis, c, step],
            yr_sem.at[axis, c, owner], *across(axis, peer),
        )

    lax.fori_loop(0, 2, scan_line, 0)
    for axis in range(2):
        every(axis, lambda step, peer: token_copy(axis, step, peer, mine(axis)).wait_send())

    def arrive(axis, c, _):
        every(axis, lambda step, peer: result_copy(axis, c, step, peer, peer).wait_recv())
        return 0

    lax.fori_loop(0, chunks, lambda c, _: arrive(0, c, _), 0)
    for c in range(chunks):
        arrive(1, c, 0)

        def widen(j, _):
            for k in range(per):
                cf_ref[c * per + k, tile(j), :] = land_ref[1, c, j, :, cols(k)].astype(F32)
            return 0

        lax.fori_loop(0, tc, widen, 0)

    def finish(r, _):
        other = jnp.concatenate([cf_ref[k, pl.ds(r, tc, stride=tr), :] for k in range(groups)], axis=1)
        v = jnp.concatenate([land_ref[0, c, r] for c in range(chunks)], axis=1).astype(F32) + other
        v = v - jnp.mean(v, axis=-1, keepdims=True)
        v = v * lax.rsqrt(jnp.mean(v * v, axis=-1, keepdims=True) + 1e-05) * og_ref[...].reshape(1, width)
        go_ref[tile(r), :] = (v * gate_ref[tile(r), :]).astype(BF16)
        return 0

    lax.fori_loop(0, tr, finish, 0)
    out_ref[...] = dot(go_ref[...], wo_ref[...]).astype(BF16).reshape(out_ref.shape)

    def sent(c, _):
        for axis in range(2):
            every(axis, lambda step, peer: result_copy(axis, c, step, peer, mine(axis)).wait_send())
        return 0

    lax.fori_loop(0, chunks, sent, 0)


def local(
    n, features, norm_gain, in_weight, conv_weight, conv_bias, proj_weight, step_weight, step_bias,
    decay_log, skip_gain, out_gain, out_weight,
):
    tr, tc, channels = features.shape
    width = out_weight.shape[0]
    tokens = tr * tc
    groups = width // LANES
    length = tc * n
    dma = pltpu.SemaphoreType.DMA
    pw = jnp.swapaxes(proj_weight, 1, 2)
    dl = jnp.swapaxes(decay_log, 1, 2)
    parts, states = pw.shape[1], dl.shape[1]
    span, per = 16, 2
    chunks = groups // per
    hbm = pl.BlockSpec(memory_space=pl.ANY)
    like = lambda a: pltpu.VMEM(a.shape, a.dtype)
    return pl.pallas_call(
        functools.partial(block_kernel, n, per),
        out_shape=jax.ShapeDtypeStruct(features.shape, BF16),
        in_specs=[hbm, VMEM, hbm, VMEM, VMEM, hbm, hbm, VMEM, hbm, VMEM, VMEM, hbm],
        out_specs=VMEM,
        scratch_shapes=[
            like(features), like(in_weight), like(pw), like(step_weight), like(dl), like(out_weight),
            pltpu.VMEM((tokens, channels), BF16),
            pltpu.VMEM((channels // LANES, tokens, LANES), F32),
            pltpu.VMEM((2, tr, channels), BF16),
            pltpu.VMEM((8 * tc, channels), BF16),
            pltpu.VMEM((groups, tr + 2, tc + 16, LANES), F32),
            pltpu.VMEM((tr, tc, width), BF16),
            pltpu.VMEM((tc, tr, width), BF16),
            pltpu.VMEM((groups, tokens, LANES), F32),
            pltpu.VMEM((2, length, width), BF16),
            pltpu.VMEM((tokens, width), F32),
            pltpu.VMEM((2, length, parts), BF16),
            pltpu.VMEM((2, length, parts), BF16),
            pltpu.VMEM((2, groups, length, LANES), F32),
            pltpu.VMEM((2, groups, length, LANES), F32),
            pltpu.VMEM((2, length * states, LANES), F32),
            pltpu.VMEM((2, length, span * states), BF16),
            pltpu.VMEM((dl.shape[0], groups, states, LANES), F32),
            pltpu.VMEM((2, per, span * states, LANES), BF16),
            pltpu.VMEM((2, per, span * states, LANES), BF16),
            pltpu.VMEM((chunks, length, per * LANES), F32),
            pltpu.VMEM((2, chunks, length, per * LANES), BF16),
            pltpu.VMEM((2, chunks, n, tc, per * LANES), BF16),
            pltpu.VMEM((groups, tokens, LANES), F32),
            pltpu.VMEM((tokens, width), BF16),
            dma((6,)), dma((8,)), dma((8,)), dma((2, n)), dma((2, n)), dma((2, chunks, n)), dma((2, chunks, n)),
        ],
        compiler_params=pltpu.CompilerParams(collective_id=0, has_side_effects=True, vmem_limit_bytes=60 << 20),
    )(
        features, norm_gain, in_weight, conv_weight, conv_bias, pw, step_weight, step_bias, dl, skip_gain,
        out_gain, out_weight,
    )


def solution(mesh):
    n = mesh.shape["row"]
    assert mesh.shape["col"] == n
    in_specs = (P("row", "col", None), P(), P(), P(), P(), P(), P(), P(), P(), P(), P(), P())
    return jax.shard_map(
        functools.partial(local, n), mesh=mesh, in_specs=in_specs, out_specs=P("row", "col", None), check_vma=False
    )
```

time: 94.2 us -> 75.3 us (0.80)
  the two profiles are of different devices: /device:TPU:1 before, /device:TPU:7 now
where the time goes in v1:
time: 75.3 us; the launch traced here: 75.1 us
  Pallas kernels  73.5 us (98%)
  local copies, waits for them, and re-layouts  1.62 us (2%)
    pallas_call x1, Pallas kernels, local(): pl.pallas_call(functools.partial(block_kernel, n, per), out_shape=jax.Sha...  73.5 us
    unnamed x1, local copies, waits for them, and re-layouts  1.62 us

profile of v1, /device:TPU:7, one launch (start us, length us, event | category | flops | bytes accessed | tf_op | source)
XLA Modules:
  0.0 75.1 jit_solution(16398433595621135782)
XLA Ops:
  0.0 73.5 %shard_map.118 = bf16[16,16,384]{2,1,0:T(8,128)(2,1)} custom-call(bf16[16,16,384]{2,1,0:T(8,128)(2,1)} %x_hbm.1, f32[384]{0:T(512)} %gain_ref.1, bf16[384,1536]{1,0:T(8,128)(2,1)} %wi_hbm.1, f32[3,3,768]{2,1,0:T(4,128)} %cw_ref.1, f32[768]{0:T(1024)} %cb_ref.1, bf16[4,56,768]{2,1,0:T(8,128)(2,1)} %bitcast.2, f32[4,24,768]{2,1,0:T(8,128)} %sw_hbm.1, ...), custom_call_target="tpu_custom_call" | custom-call | tf_op jit(solution)/shard_map/pallas_call | solution.py:415
  73.5 1.6 %copy.14 = bf16[16,16,384]{2,1,0:T(8,128)(2,1)} copy(bf16[16,16,384]{2,1,0:T(8,128)(2,1)} %shard_map.118) | data formatting | bytes 393216

commit v2 on v1

--- a/solution.py
+++ b/solution.py
@@ -13,6 +13,7 @@
 NT = (((1,), (1,)), ((), ()))
 LANES = 128
 LOG2E = 1.4426950408889634
+PIECE = 2
 VMEM = pl.BlockSpec(memory_space=pltpu.VMEM)
 
 
@@ -80,7 +81,7 @@
     n, per, x_hbm, gain_ref, wi_hbm, cw_ref, cb_ref, pw_hbm, sw_hbm, sb_ref, dl_hbm, sk_ref, og_ref, wo_hbm, out_ref,
     x_ref, wi_ref, pw_ref, sw_ref, dl_ref, wo_ref,
     nb_ref, nf_ref, strip_ref, halo_ref, pad_ref, act_ref, actt_ref, actf_ref, line_ref, gate_ref,
-    ph_ref, pl_ref, s_ref, du_ref, bb_ref, mc_ref, dec_ref, ha_ref, hb_ref, acc_ref, y_ref, land_ref, cf_ref, go_ref,
+    s_ref, du_ref, bb_ref, mc_ref, dec_ref, ha_ref, hb_ref, acc_ref, y_ref, land_ref, cf_ref, go_ref,
     own_sem, hs_sem, hr_sem, ts_sem, tr_sem, ys_sem, yr_sem,
 ):
     tr, tc, channels = x_ref.shape
@@ -90,7 +91,7 @@
     chunks = groups // per
     chunk = per * LANES
     length = line_ref.shape[1]
-    rank, states, parts = sw_ref.shape[1], dl_ref.shape[1], pw_ref.shape[1]
+    rank, states = sw_ref.shape[1], dl_ref.shape[1]
     row, col = place()
     fetch = [
         pltpu.make_async_copy(src, dst, own_sem.at[i])
@@ -141,6 +142,33 @@
     left, right = strip_ref.at[0], strip_ref.at[1]
     up, down = lax.rem(row + n - 1, n), lax.rem(row + 1, n)
     west, east = lax.rem(col + n - 1, n), lax.rem(col + 1, n)
+    fetch[1].wait()
+
+    def project(i, _):
+        at = pl.ds(pl.multiple_of(i * step, step), step)
+        inner = dot(nb_ref[at, :], wi_ref[:, :width]).astype(BF16).astype(F32)
+        for k in range(groups):
+            pad_ref[k, pl.ds(1 + i * 4, 4), 8 : 8 + tc, :] = inner[:, cols(k)].reshape(4, tc, LANES)
+        return 0
+
+    lax.fori_loop(0, tokens // step, project, 0)
+
+    def gates(i, _):
+        at = pl.ds(pl.multiple_of(i * step, step), step)
+        gate = dot(nb_ref[at, :], wi_ref[:, width:]).astype(BF16).astype(F32)
+        gate_ref[at, :] = silu(gate)
+        return 0
+
+    lax.fori_loop(0, tokens // step, gates, 0)
+    for i in (2, 3, 4, 5):
+        fetch[i].wait()
+
+    def rates(d, _):
+        for k in range(groups):
+            dec_ref[d, k] = jnp.exp(dl_ref[d, :, cols(k)]) * -LOG2E
+        return 0
+
+    lax.fori_loop(0, dl_ref.shape[0], rates, 0)
     greeted()
     plan = (
         (bottom, down, col), (top, up, col), (right, row, east), (left, row, west),
@@ -152,16 +180,6 @@
     ]
     for copy in halos:
         copy.start()
-    fetch[1].wait()
-
-    def project(i, _):
-        at = pl.ds(pl.multiple_of(i * step, step), step)
-        inner = dot(nb_ref[at, :], wi_ref[:, :width]).astype(BF16).astype(F32)
-        for k in range(groups):
-            pad_ref[k, pl.ds(1 + i * 4, 4), 8 : 8 + tc, :] = inner[:, cols(k)].reshape(4, tc, LANES)
-        return 0
-
-    lax.fori_loop(0, tokens // step, project, 0)
     for copy in halos:
         copy.wait()
     edge = dot(halo_ref[...], wi_ref[:, :width]).astype(BF16).astype(F32)
@@ -220,47 +238,41 @@
         return 0
 
     lax.fori_loop(0, tc, flip, 0)
-    every(1, lambda step, peer: token_copy(1, step, peer, row).start())
     line_ref[0, tile(col), :] = act_ref[col]
     line_ref[1, tile(row), :] = actt_ref[row]
-
-    def gates(i, _):
-        at = pl.ds(pl.multiple_of(i * step, step), step)
-        gate = dot(nb_ref[at, :], wi_ref[:, width:]).astype(BF16).astype(F32)
-        gate_ref[at, :] = silu(gate)
-        return 0
-
-    lax.fori_loop(0, tokens // step, gates, 0)
-    fetch[4].wait()
-
-    def rates(d, _):
-        for k in range(groups):
-            dec_ref[d, k] = jnp.exp(dl_ref[d, :, cols(k)]) * -LOG2E
-        return 0
-
-    lax.fori_loop(0, dl_ref.shape[0], rates, 0)
-    for i in (2, 3, 5):
-        fetch[i].wait()
 
     span = 16
     blocks = length // span
     held = (ha_ref, hb_ref)
-    kk, cc = iota((parts, span * states), 0), iota((parts, span * states), 1)
+    kk, cc = iota((3 * rank + states, span * states), 0), iota((3 * rank + states, span * states), 1)
     lane = iota((states, LANES), 1)
 
-    def scan_line(line, _):
-        every(line, lambda step, peer: token_arrival(line, step, peer))
+    def scan_line(line):
 
         def prepare(d, _):
             which = line * 2 + d
-            repeat = (kk == rank + states + lax.rem(cc, states)).astype(BF16)
+            repeat = (kk == 3 * rank + lax.rem(cc, states)).astype(BF16)
             mask = lax.rem(iota((length, span * states), 0), span) == iota((length, span * states), 1) // states
             u = line_ref[line]
-            p = dot_nt(u, pw_ref[which])
+            to_rank = pw_ref[which, :rank, :]
+            p = dot_nt(u, jnp.concatenate([to_rank] * 3 + [pw_ref[which, rank + states :, :]], axis=0))
             high = p.astype(BF16)
-            ph_ref[d] = high
-            pl_ref[d] = (p - high.astype(F32)).astype(BF16)
+            low = p - high.astype(F32)
+            stacked = jnp.where(iota(p.shape, 1) < 2 * rank, high.astype(F32), low).astype(BF16)[:, : 3 * rank]
             mc_ref[d] = jnp.where(mask, dot(high, repeat), 0.0).astype(BF16)
+            weight = sw_ref[which]
+            swh = weight.astype(BF16)
+            swl = (weight - swh.astype(F32)).astype(BF16)
+            weights = jnp.concatenate([swh, swl, swh], axis=0)
+            shift = sb_ref[pl.ds(which, 1), :]
+            wide = PIECE * LANES
+            for g in range(0, groups, PIECE):
+                at = slice(g * LANES, g * LANES + wide)
+                s = softplus(dot(stacked, weights[:, at]) + shift[:, at])
+                du = s * line_ref[line, :, at].astype(F32)
+                for k in range(PIECE):
+                    s_ref[d, g + k] = s[:, cols(k)]
+                    du_ref[d, g + k] = du[:, cols(k)]
             enter = dot_nt(pw_ref[which, rank : rank + states, :], u)
             ones = jnp.ones((LANES, LANES), BF16)
             for h in range(length // LANES):
@@ -268,22 +280,6 @@
                     spread = [jnp.where(lane == g + i, enter[:, cols(h)], 0.0) for i in range(span)]
                     at = (h * LANES + g) * states
                     bb_ref[d, at : at + span * states, :] = dot(jnp.concatenate(spread, axis=0).astype(BF16), ones)
-            weight = sw_ref[which]
-            swh = weight.astype(BF16)
-            swl = (weight - swh.astype(F32)).astype(BF16)
-            shift = sb_ref[pl.ds(which, 1), :]
-
-            def step_size(i, _):
-                at = pl.ds(pl.multiple_of(i * 32, 32), 32)
-                a = ph_ref[d, at, :rank]
-                s = softplus(dot(a, swh) + (dot(a, swl) + dot(pl_ref[d, at, :rank], swh)) + shift)
-                du = s * line_ref[line, at, :].astype(F32)
-                for k in range(groups):
-                    s_ref[d, k, at, :] = s[:, cols(k)]
-                    du_ref[d, k, at, :] = du[:, cols(k)]
-                return 0
-
-            lax.fori_loop(0, length // 32, step_size, 0)
             return 0
 
         lax.fori_loop(0, 2, prepare, 0)
@@ -349,7 +345,6 @@
             return 0
 
         lax.fori_loop(0, chunks, scan_chunk, 0)
-        return 0
 
     def result_copy(axis, c, step, peer, owner):
         return remote(
@@ -357,7 +352,11 @@
             yr_sem.at[axis, c, owner], *across(axis, peer),
         )
 
-    lax.fori_loop(0, 2, scan_line, 0)
+    every(0, lambda step, peer: token_arrival(0, step, peer))
+    every(1, lambda step, peer: token_copy(1, step, peer, row).start())
+    scan_line(0)
+    every(1, lambda step, peer: token_arrival(1, step, peer))
+    scan_line(1)
     for axis in range(2):
         every(axis, lambda step, peer: token_copy(axis, step, peer, mine(axis)).wait_send())
 
@@ -407,8 +406,8 @@
     dma = pltpu.SemaphoreType.DMA
     pw = jnp.swapaxes(proj_weight, 1, 2)
     dl = jnp.swapaxes(decay_log, 1, 2)
-    parts, states = pw.shape[1], dl.shape[1]
-    span, per = 16, 2
+    states = dl.shape[1]
+    span, per = 16, 3
     chunks = groups // per
     hbm = pl.BlockSpec(memory_space=pl.ANY)
     like = lambda a: pltpu.VMEM(a.shape, a.dtype)
@@ -429,8 +428,6 @@
             pltpu.VMEM((groups, tokens, LANES), F32),
             pltpu.VMEM((2, length, width), BF16),
             pltpu.VMEM((tokens, width), F32),
-            pltpu.VMEM((2, length, parts), BF16),
-            pltpu.VMEM((2, length, parts), BF16),
             pltpu.VMEM((2, groups, length, LANES), F32),
             pltpu.VMEM((2, groups, length, LANES), F32),
             pltpu.VMEM((2, length * states, LANES), F32),

time: 75.3 us -> 64.6 us (0.86)
  the two profiles are of different devices: /device:TPU:7 before, /device:TPU:1 now
where the time goes in v2:
time: 64.6 us; the launch traced here: 64.4 us
  Pallas kernels  62.7 us (97%)
  local copies, waits for them, and re-layouts  1.62 us (3%)
    pallas_call x1, Pallas kernels, local(): pl.pallas_call(functools.partial(block_kernel, n, per), out_shape=jax.Sha...  62.7 us
    unnamed x1, local copies, waits for them, and re-layouts  1.62 us

profile of v2, /device:TPU:1, one launch (start us, length us, event | category | flops | bytes accessed | tf_op | source)
XLA Modules:
  0.0 64.4 jit_solution(7465585146836263933)
XLA Ops:
  0.0 62.7 %shard_map.118 = bf16[16,16,384]{2,1,0:T(8,128)(2,1)} custom-call(bf16[16,16,384]{2,1,0:T(8,128)(2,1)} %x_hbm.1, f32[384]{0:T(512)} %gain_ref.1, bf16[384,1536]{1,0:T(8,128)(2,1)} %wi_hbm.1, f32[3,3,768]{2,1,0:T(4,128)} %cw_ref.1, f32[768]{0:T(1024)} %cb_ref.1, bf16[4,56,768]{2,1,0:T(8,128)(2,1)} %bitcast.2, f32[4,24,768]{2,1,0:T(8,128)} %sw_hbm.1, ...), custom_call_target="tpu_custom_call" | custom-call | tf_op jit(solution)/shard_map/pallas_call | solution.py:414
  62.8 1.6 %copy.14 = bf16[16,16,384]{2,1,0:T(8,128)(2,1)} copy(bf16[16,16,384]{2,1,0:T(8,128)(2,1)} %shard_map.118) | data formatting | bytes 393216

commit v3 on v2

v3 whole, which is shorter than its diff:
```python
import functools

import jax
import jax.numpy as jnp
from jax import lax
from jax.experimental import pallas as pl
from jax.experimental.pallas import tpu as pltpu
from jax.sharding import PartitionSpec as P

F32 = jnp.float32
BF16 = jnp.bfloat16
MESH = pl.DeviceIdType.MESH
NT = (((1,), (1,)), ((), ()))
LANES = 128
LOG2E = 1.4426950408889634
PIECE = 2
PER = (3, 2)
VMEM = pl.BlockSpec(memory_space=pltpu.VMEM)


def dot(a, b):
    return jnp.dot(a, b, preferred_element_type=F32)


def dot_nt(a, b):
    return lax.dot_general(a, b, NT, preferred_element_type=F32)


def softplus(z):
    w = jnp.exp2(jnp.abs(z) * -LOG2E)
    small = w * (1.0 - w * (0.5 - w * (1.0 / 3.0)))
    return jnp.maximum(z, 0.0) + jnp.where(w < 0.01, small, jnp.log(1.0 + w))


def silu(v):
    return v / (1.0 + jnp.exp(-v))


def iota(shape, dim):
    return lax.broadcasted_iota(jnp.int32, shape, dim)


def cols(k):
    return slice(k * LANES, (k + 1) * LANES)


def place():
    return lax.axis_index("row"), lax.axis_index("col")


def greet(nr, nc):
    row, col = place()
    sem = pltpu.get_barrier_semaphore()

    def signal(r, c):
        pl.semaphore_signal(sem, inc=1, device_id={"row": r, "col": c}, device_id_type=MESH)

    def along_col(k, _):
        signal(row, lax.rem(col + k, nc))
        return 0

    def along_row(k, _):
        signal(lax.rem(row + k, nr), col)
        return 0

    lax.fori_loop(1, nc, along_col, 0)
    lax.fori_loop(1, nr, along_row, 0)
    for dr in (1, nr - 1):
        for dc in (1, nc - 1):
            signal(lax.rem(row + dr, nr), lax.rem(col + dc, nc))
    return lambda: pl.semaphore_wait(sem, nr + nc + 2)


def remote(src, dst, send_sem, recv_sem, r, c):
    return pltpu.make_async_remote_copy(
        src_ref=src, dst_ref=dst, send_sem=send_sem, recv_sem=recv_sem,
        device_id={"row": r, "col": c}, device_id_type=MESH,
    )


def block_kernel(
    n, x_hbm, gain_hbm, wi_hbm, cw_hbm, cb_hbm, pw_hbm, sw_hbm, sb_hbm, dl_hbm, sk_hbm, og_hbm, wo_hbm, out_ref,
    x_ref, gain_ref, wi_ref, cw_ref, cb_ref, pw_ref, sw_ref, sb_ref, dl_ref, sk_ref, og_ref, wo_ref,
    nb_ref, nf_ref, strip_ref, halo_ref, pad_ref, act_ref, actt_ref, actf_ref, line_ref, gate_ref,
    s_ref, du_ref, bb_ref, mc_ref, dec_ref, ha_ref, hb_ref, acc_ref, y_ref, land_ref, cf_ref, go_ref,
    st_ref, sl_ref, own_sem, hs_sem, hr_sem, ts_sem, tr_sem, ys_sem, yr_sem, ss_sem, sr_sem,
):
    tr, tc, channels = x_ref.shape
    width = cb_ref.shape[-1]
    tokens = tr * tc
    groups = width // LANES
    length = line_ref.shape[1]
    rank, states = sw_ref.shape[1], dl_ref.shape[1]
    row, col = place()
    there = (x_hbm, gain_hbm, wi_hbm, cw_hbm, cb_hbm, pw_hbm, sw_hbm, sb_hbm, dl_hbm, sk_hbm, og_hbm, wo_hbm)
    here = (x_ref, gain_ref, wi_ref, cw_ref, cb_ref, pw_ref, sw_ref, sb_ref, dl_ref, sk_ref, og_ref, wo_ref)
    fetch = [pltpu.make_async_copy(src, dst, own_sem.at[i]) for i, (src, dst) in enumerate(zip(there, here))]
    for copy in fetch:
        copy.start()
    greeted = greet(n, n)

    half = n // 2
    side, seat = col // half, lax.rem(col, half)

    def others(one):
        def body(step, _):
            one(step, lax.rem(row + step, n))
            return 0

        lax.fori_loop(1, n, body, 0)

    def mates(one):
        def body(step, _):
            r = lax.rem(2 * seat + step, n)
            one(r, r // 2, lax.rem(r, 2))
            return 0

        lax.fori_loop(2, n, body, 0)

    def tile(i):
        return pl.ds(pl.multiple_of(i * tc, tc), tc)

    step = 4 * tc
    fetch[0].wait()
    fetch[1].wait()

    def norm(i, _):
        v = x_ref[pl.ds(i * 4, 4)].reshape(step, channels).astype(F32)
        v = v - jnp.mean(v, axis=-1, keepdims=True)
        v = v * lax.rsqrt(jnp.mean(v * v, axis=-1, keepdims=True) + 1e-05) * gain_ref[...].reshape(1, channels)
        at = pl.ds(pl.multiple_of(i * step, step), step)
        nb_ref[at, :] = v.astype(BF16)
        for k in range(channels // LANES):
            nf_ref[k, at, :] = v[:, cols(k)]
        return 0

    lax.fori_loop(0, tokens // step, norm, 0)
    for k in range(channels // LANES):
        strip_ref[0, :, cols(k)] = nf_ref[k, pl.ds(0, tr, stride=tc), :].astype(BF16)
        strip_ref[1, :, cols(k)] = nf_ref[k, pl.ds(tc - 1, tr, stride=tc), :].astype(BF16)
    top, bottom = nb_ref.at[pl.ds(0, tc)], nb_ref.at[pl.ds(tokens - tc, tc)]
    left, right = strip_ref.at[0], strip_ref.at[1]
    up, down = lax.rem(row + n - 1, n), lax.rem(row + 1, n)
    west, east = lax.rem(col + n - 1, n), lax.rem(col + 1, n)
    greeted()
    plan = (
        (bottom, down, col), (top, up, col), (right, row, east), (left, row, west),
        (bottom, down, east), (bottom, down, west), (top, up, east), (top, up, west),
    )
    halos = [
        remote(src, halo_ref.at[pl.ds(slot * tc, tc)], hs_sem.at[slot], hr_sem.at[slot], r, c)
        for slot, (src, r, c) in enumerate(plan)
    ]
    for copy in halos:
        copy.start()
    fetch[2].wait()

    def project(i, _):
        at = pl.ds(pl.multiple_of(i * step, step), step)
        inner = dot(nb_ref[at, :], wi_ref[:, :width]).astype(BF16).astype(F32)
        for k in range(groups):
            pad_ref[k, pl.ds(1 + i * 4, 4), 8 : 8 + tc, :] = inner[:, cols(k)].reshape(4, tc, LANES)
        return 0

    lax.fori_loop(0, tokens // step, project, 0)
    for copy in halos:
        copy.wait()
    edge = dot(halo_ref[...], wi_ref[:, :width]).astype(BF16).astype(F32)
    north, south = row > 0, row < n - 1
    lwest, least = col > 0, col < n - 1

    def seen(slot, ok, first=0, count=tc):
        return jnp.where(ok, edge[slot * tc + first : slot * tc + first + count], 0.0)

    n_all, s_all = seen(0, north), seen(1, south)
    w_all, e_all = seen(2, lwest), seen(3, least)
    nw, ne = seen(4, north & lwest, tc - 8, 8), seen(5, north & least, 0, 8)
    sw, se = seen(6, south & lwest, tc - 8, 8), seen(7, south & least, 0, 8)
    for k in range(groups):
        pad_ref[k, 0, 8 : 8 + tc, :] = n_all[:, cols(k)]
        pad_ref[k, tr + 1, 8 : 8 + tc, :] = s_all[:, cols(k)]
        pad_ref[k, 0, 0:8, :] = nw[:, cols(k)]
        pad_ref[k, 0, 8 + tc : 16 + tc, :] = ne[:, cols(k)]
        pad_ref[k, tr + 1, 0:8, :] = sw[:, cols(k)]
        pad_ref[k, tr + 1, 8 + tc : 16 + tc, :] = se[:, cols(k)]
        for r in range(tr):
            pad_ref[k, 1 + r, 7:8, :] = w_all[r : r + 1, cols(k)]
            pad_ref[k, 1 + r, 8 + tc : 9 + tc, :] = e_all[r : r + 1, cols(k)]
    fetch[3].wait()
    fetch[4].wait()
    bias = cb_ref[...].reshape(1, width)

    def row_tokens(r, to, which, owner):
        return remote(
            act_ref.at[r], line_ref.at[0, tile(which * half + owner)], ts_sem.at[0, r],
            tr_sem.at[0, which * half + owner], row, side * half + to,
        )

    def column_tokens(step, peer, owner):
        return remote(actt_ref.at[peer], line_ref.at[1, tile(owner)], ts_sem.at[1, step], tr_sem.at[1, owner], peer, col)

    def convolve(i, _):
        r = lax.rem(2 * seat + i, n)
        for k in range(groups):
            total = jnp.broadcast_to(bias[:, cols(k)], (tc, LANES))
            for a in range(3):
                for b in range(3):
                    total = total + pad_ref[k, r + a, 7 + b : 7 + b + tc, :] * cw_ref[a, b : b + 1, cols(k)]
            done = silu(total).astype(BF16)
            act_ref[r, :, cols(k)] = done
            actf_ref[k, tile(r), :] = done.astype(F32)

        @pl.when(i < n)
        def _():
            row_tokens(r, r // 2, lax.rem(r, 2), seat).start()

        return 0

    lax.fori_loop(2, n + 2, convolve, 0)

    def flip(j, _):
        for k in range(groups):
            actt_ref[j, :, cols(k)] = actf_ref[k, pl.ds(j, tr, stride=tc), :].astype(BF16)
        return 0

    lax.fori_loop(0, tc, flip, 0)
    others(lambda step, peer: column_tokens(step, peer, row).start())
    for which in range(2):
        line_ref[0, tile(which * half + seat), :] = act_ref[2 * seat + which]
    line_ref[1, tile(row), :] = actt_ref[row]

    def gates(i, _):
        at = pl.ds(pl.multiple_of(i * step, step), step)
        gate = dot(nb_ref[at, :], wi_ref[:, width:]).astype(BF16).astype(F32)
        gate_ref[at, :] = silu(gate)
        return 0

    lax.fori_loop(0, tokens // step, gates, 0)
    for i in range(5, len(fetch)):
        fetch[i].wait()

    def rates(d, _):
        for k in range(groups):
            dec_ref[d, k] = jnp.exp(dl_ref[d, :, cols(k)]) * -LOG2E
        return 0

    lax.fori_loop(0, dl_ref.shape[0], rates, 0)

    span = 16
    blocks = length // span
    held = (ha_ref, hb_ref)
    kk, cc = iota((3 * rank + states, span * states), 0), iota((3 * rank + states, span * states), 1)
    lane = iota((states, LANES), 1)

    def ready(line):
        def prepare(d, _):
            which = line * 2 + d
            repeat = (kk == 3 * rank + lax.rem(cc, states)).astype(BF16)
            slot = iota((length, span * states), 1) // states
            mask = lax.rem(iota((length, span * states), 0), span) == slot + d * (span - 1 - 2 * slot)
            u = line_ref[line]
            to_rank = pw_ref[which, :rank, :]
            p = dot_nt(u, jnp.concatenate([to_rank] * 3 + [pw_ref[which, rank + states :, :]], axis=0))
            high = p.astype(BF16)
            low = p - high.astype(F32)
            stacked = jnp.where(iota(p.shape, 1) < 2 * rank, high.astype(F32), low).astype(BF16)[:, : 3 * rank]
            mc_ref[d] = jnp.where(mask, dot(high, repeat), 0.0).astype(BF16)
            weight = sw_ref[which]
            swh = weight.astype(BF16)
            swl = (weight - swh.astype(F32)).astype(BF16)
            weights = jnp.concatenate([swh, swl, swh], axis=0)
            shift = sb_ref[pl.ds(which, 1), :]
            wide = PIECE * LANES
            for g in range(0, groups, PIECE):
                at = slice(g * LANES, g * LANES + wide)
                s = softplus(dot(stacked, weights[:, at]) + shift[:, at])
                du = s * line_ref[line, :, at].astype(F32)
                for k in range(PIECE):
                    s_ref[d, g + k] = s[:, cols(k)]
                    du_ref[d, g + k] = du[:, cols(k)]
            enter = dot_nt(pw_ref[which, rank : rank + states, :], u)
            ones = jnp.ones((LANES, LANES), BF16)
            for h in range(length // LANES):
                for g in range(0, LANES, span):
                    spread = [jnp.where(lane == g + i, enter[:, cols(h)], 0.0) for i in range(span)]
                    at = (h * LANES + g) * states
                    bb_ref[d, at : at + span * states, :] = dot(jnp.concatenate(spread, axis=0).astype(BF16), ones)
            return 0

        lax.fori_loop(0, 2, prepare, 0)
        skip = sk_ref[pl.ds(line * 2, 1), :] + sk_ref[pl.ds(line * 2 + 1, 1), :]

        def begin(i, _):
            at = pl.ds(pl.multiple_of(i * 32, 32), 32)
            v = line_ref[line, at, :].astype(F32) * skip
            for k in range(groups):
                acc_ref[k, at, :] = v[:, cols(k)]
            return 0

        lax.fori_loop(0, length // 32, begin, 0)

    def zeros(per):
        return tuple(tuple((jnp.zeros((8, LANES), F32),) * 2 for _ in range(per)) for _ in range(2))

    def run(per, g0, streams, blocks, init):
        dec = [
            [[dec_ref[w, g0 + k, 8 * v : 8 * v + 8, :] for v in range(2)] for k in range(per)] for w, _, _, _ in streams
        ]

        def low(i, q):
            _, _, first, back = streams[q]
            return pl.multiple_of(first + (i + back * (blocks - 1 - 2 * i)) * span, span)

        def leave(slot, i, q):
            b = low(i, q)
            states_now = jnp.concatenate([held[slot][q, k] for k in range(per)], axis=1)
            part = dot(mc_ref[streams[q][1], pl.ds(b, span), :], states_now)
            for k in range(per):
                acc_ref[g0 + k, pl.ds(b, span), :] += part[:, cols(k)]

        def advance(slot, i, h):
            for j in range(span):
                for q in range(2):
                    _, d, _, back = streams[q]
                    t = low(i, q) + (j + back * (span - 1 - 2 * j))
                    enter = [bb_ref[d, pl.ds(pl.multiple_of(t * states + 8 * v, 8), 8), :] for v in range(2)]
                    for k in range(per):
                        s = s_ref[d, g0 + k, pl.ds(t, 8, stride=0), :]
                        du = du_ref[d, g0 + k, pl.ds(t, 8, stride=0), :]
                        now = [jnp.exp2(s * dec[q][k][v]) * h[q][k][v] + du * enter[v] for v in range(2)]
                        h[q][k] = now
                        held[slot][q, k, j * states : (j + 1) * states, :] = jnp.concatenate(now, axis=0).astype(BF16)
            return h

        def body(i, h):
            h = [[list(v) for v in part] for part in h]
            for q in range(2):
                leave(1, jnp.maximum(2 * i - 1, 0), q)
            h = advance(0, 2 * i, h)
            for q in range(2):
                leave(0, 2 * i, q)
            h = advance(1, 2 * i + 1, h)
            return tuple(tuple(tuple(v) for v in part) for part in h)

        for q in range(2):
            for k in range(per):
                hb_ref[q, k] = jnp.zeros_like(hb_ref[q, k])
        h = lax.fori_loop(0, blocks // 2, body, init)
        for q in range(2):
            leave(1, blocks - 1, q)
        return h

    def settle(line, per, g0):
        for k in range(per):
            y_ref[line, g0 + k] = acc_ref[g0 + k].astype(BF16)

    def row_result(c, r, to, which, owner):
        at = pl.ds(c * PER[0], PER[0])
        return remote(
            y_ref.at[0, at, tile(which * half + to)], land_ref.at[0, at, 2 * owner + which], ys_sem.at[0, c, r],
            yr_sem.at[0, c, 2 * owner + which], row, side * half + to,
        )

    def column_result(c, step, peer, owner):
        at = pl.ds(c * PER[1], PER[1])
        return remote(
            y_ref.at[1, at, tile(peer)], land_ref.at[1, at, owner], ys_sem.at[1, c, step], yr_sem.at[1, c, owner],
            peer, col,
        )

    def state_copy(c):
        return remote(st_ref.at[c], sl_ref.at[c], ss_sem.at[c], sr_sem.at[c], row, lax.rem(col + half, n))

    def lines(d):
        return [(d, d, which * (length // 2), d) for which in range(2)]

    def outward(c, _):
        per = PER[0]
        h = run(per, c * per, lines(side), blocks // 2, zeros(per))
        for q in range(2):
            for k in range(per):
                st_ref[c, q, k] = jnp.concatenate(h[q][k], axis=0).astype(BF16)
        state_copy(c).start()
        return 0

    def inward(c, _):
        per = PER[0]
        state_copy(c).wait_recv()
        came = [[sl_ref[c, q, k].astype(F32) for k in range(per)] for q in range(2)]
        init = tuple(tuple((v[:8], v[8:]) for v in part) for part in came)
        run(per, c * per, lines(1 - side), blocks // 2, init)
        settle(0, per, c * per)
        mates(lambda r, to, which: row_result(c, r, to, which, seat).start())
        for k in range(per):
            for which in range(2):
                land_ref[0, c * per + k, 2 * seat + which] = y_ref[0, c * per + k, tile(which * half + seat), :]
        return 0

    def down_and_up(c, _):
        per = PER[1]
        run(per, c * per, [(2, 0, 0, 0), (3, 1, 0, 1)], blocks, zeros(per))
        settle(1, per, c * per)
        others(lambda step, peer: column_result(c, step, peer, row).start())
        for k in range(per):
            land_ref[1, c * per + k, row] = y_ref[1, c * per + k, tile(row), :]
        return 0

    mates(lambda r, to, which: row_tokens(r, to, which, to).wait_recv())
    ready(0)
    lax.fori_loop(0, groups // PER[0], outward, 0)
    lax.fori_loop(0, groups // PER[0], inward, 0)
    others(lambda step, peer: column_tokens(step, peer, peer).wait_recv())
    ready(1)
    lax.fori_loop(0, groups // PER[1], down_and_up, 0)
    mates(lambda r, to, which: row_tokens(r, to, which, seat).wait_send())
    others(lambda step, peer: column_tokens(step, peer, row).wait_send())
    for c in range(groups // PER[0]):
        state_copy(c).wait_send()
        mates(lambda r, to, which: row_result(c, r, to, which, to).wait_recv())
    for c in range(groups // PER[1]):
        others(lambda step, peer: column_result(c, step, peer, peer).wait_recv())

        def widen(j, _):
            for k in range(c * PER[1], (c + 1) * PER[1]):
                cf_ref[k, tile(j), :] = land_ref[1, k, j].astype(F32)
            return 0

        lax.fori_loop(0, tc, widen, 0)

    def finish(r, _):
        other = jnp.concatenate([cf_ref[k, pl.ds(r, tc, stride=tr), :] for k in range(groups)], axis=1)
        v = jnp.concatenate([land_ref[0, k, r] for k in range(groups)], axis=1).astype(F32) + other
        v = v - jnp.mean(v, axis=-1, keepdims=True)
        v = v * lax.rsqrt(jnp.mean(v * v, axis=-1, keepdims=True) + 1e-05) * og_ref[...].reshape(1, width)
        go_ref[tile(r), :] = (v * gate_ref[tile(r), :]).astype(BF16)
        return 0

    lax.fori_loop(0, tr, finish, 0)
    out_ref[...] = dot(go_ref[...], wo_ref[...]).astype(BF16).reshape(out_ref.shape)

    for c in range(groups // PER[0]):
        mates(lambda r, to, which: row_result(c, r, to, which, seat).wait_send())
    for c in range(groups // PER[1]):
        others(lambda step, peer: column_result(c, step, peer, row).wait_send())


def local(
    n, features, norm_gain, in_weight, conv_weight, conv_bias, proj_weight, step_weight, step_bias,
    decay_log, skip_gain, out_gain, out_weight,
):
    tr, tc, channels = features.shape
    width = out_weight.shape[0]
    tokens = tr * tc
    groups = width // LANES
    length = tc * n
    dma = pltpu.SemaphoreType.DMA
    pw = jnp.swapaxes(proj_weight, 1, 2)
    dl = jnp.swapaxes(decay_log, 1, 2)
    states = dl.shape[1]
    span, per = 16, max(PER)
    chunks = groups // min(PER)
    hbm = pl.BlockSpec(memory_space=pltpu.HBM)
    operands = (
        features, norm_gain, in_weight, conv_weight, conv_bias, pw, step_weight, step_bias, dl, skip_gain,
        out_gain, out_weight,
    )
    return pl.pallas_call(
        functools.partial(block_kernel, n),
        out_shape=jax.ShapeDtypeStruct(features.shape, BF16),
        in_specs=[hbm] * len(operands),
        out_specs=VMEM,
        scratch_shapes=[pltpu.VMEM(a.shape, a.dtype) for a in operands] + [
            pltpu.VMEM((tokens, channels), BF16),
            pltpu.VMEM((channels // LANES, tokens, LANES), F32),
            pltpu.VMEM((2, tr, channels), BF16),
            pltpu.VMEM((8 * tc, channels), BF16),
            pltpu.VMEM((groups, tr + 2, tc + 16, LANES), F32),
            pltpu.VMEM((tr, tc, width), BF16),
            pltpu.VMEM((tc, tr, width), BF16),
            pltpu.VMEM((groups, tokens, LANES), F32),
            pltpu.VMEM((2, length, width), BF16),
            pltpu.VMEM((tokens, width), F32),
            pltpu.VMEM((2, groups, length, LANES), F32),
            pltpu.VMEM((2, groups, length, LANES), F32),
            pltpu.VMEM((2, length * states, LANES), F32),
            pltpu.VMEM((2, length, span * states), BF16),
            pltpu.VMEM((dl.shape[0], groups, states, LANES), F32),
            pltpu.VMEM((2, per, span * states, LANES), BF16),
            pltpu.VMEM((2, per, span * states, LANES), BF16),
            pltpu.VMEM((groups, length, LANES), F32),
            pltpu.VMEM((2, groups, length, LANES), BF16),
            pltpu.VMEM((2, groups, n, tc, LANES), BF16),
            pltpu.VMEM((groups, tokens, LANES), F32),
            pltpu.VMEM((tokens, width), BF16),
            pltpu.VMEM((groups // PER[0], 2, PER[0], states, LANES), BF16),
            pltpu.VMEM((groups // PER[0], 2, PER[0], states, LANES), BF16),
            dma((len(operands),)), dma((8,)), dma((8,)), dma((2, n)), dma((2, n)), dma((2, chunks, n)), dma((2, chunks, n)),
            dma((groups // PER[0],)), dma((groups // PER[0],)),
        ],
        compiler_params=pltpu.CompilerParams(collective_id=0, has_side_effects=True, vmem_limit_bytes=60 << 20),
    )(*operands)


def solution(mesh):
    n = mesh.shape["row"]
    assert mesh.shape["col"] == n
    in_specs = (P("row", "col", None), P(), P(), P(), P(), P(), P(), P(), P(), P(), P(), P())
    return jax.shard_map(
        functools.partial(local, n), mesh=mesh, in_specs=in_specs, out_specs=P("row", "col", None), check_vma=False
    )
```

time: 64.6 us -> 65.9 us (1.020)
  Pallas kernels: 62.7 us -> 64.2 us
    pallas_call x1, Pallas kernels: 62.7 us -> 64.2 us  [local(): pl.pallas_call(functools.partial(block_kernel, n), out_shape=jax.ShapeDty...]
where the time goes in v3:
time: 65.9 us; the launch traced here: 65.8 us
  Pallas kernels  64.2 us (97%)
  local copies, waits for them, and re-layouts  1.62 us (2%)
    pallas_call x1, Pallas kernels, local(): pl.pallas_call(functools.partial(block_kernel, n), out_shape=jax.ShapeDty...  64.2 us
    unnamed x1, local copies, waits for them, and re-layouts  1.62 us

profile of v3, /device:TPU:1, one launch (start us, length us, event | category | flops | bytes accessed | tf_op | source)
XLA Modules:
  0.0 65.8 jit_solution(3078197225476622836)
XLA Ops:
  0.0 64.2 %shard_map.118 = bf16[16,16,384]{2,1,0:T(8,128)(2,1)} custom-call(bf16[16,16,384]{2,1,0:T(8,128)(2,1)} %x_hbm.1, f32[384]{0:T(512)} %gain_hbm.1, bf16[384,1536]{1,0:T(8,128)(2,1)} %wi_hbm.1, f32[3,3,768]{2,1,0:T(4,128)} %cw_hbm.1, f32[768]{0:T(1024)} %cb_hbm.1, bf16[4,56,768]{2,1,0:T(8,128)(2,1)} %bitcast.2, f32[4,24,768]{2,1,0:T(8,128)} %sw_hbm.1, ...), custom_call_target="tpu_custom_call" | custom-call | tf_op jit(solution)/shard_map/pallas_call | solution.py:467
  64.2 1.6 %copy.14 = bf16[16,16,384]{2,1,0:T(8,128)(2,1)} copy(bf16[16,16,384]{2,1,0:T(8,128)(2,1)} %shard_map.118) | data formatting | bytes 393216

commit v4 on v3

--- a/solution.py
+++ b/solution.py
@@ -14,7 +14,7 @@
 LANES = 128
 LOG2E = 1.4426950408889634
 PIECE = 2
-PER = (3, 2)
+PER = (3, 3)
 VMEM = pl.BlockSpec(memory_space=pltpu.VMEM)
 
 
@@ -264,7 +264,7 @@
             high = p.astype(BF16)
             low = p - high.astype(F32)
             stacked = jnp.where(iota(p.shape, 1) < 2 * rank, high.astype(F32), low).astype(BF16)[:, : 3 * rank]
-            mc_ref[d] = jnp.where(mask, dot(high, repeat), 0.0).astype(BF16)
+            mc_ref[line, d] = jnp.where(mask, dot(high, repeat), 0.0).astype(BF16)
             weight = sw_ref[which]
             swh = weight.astype(BF16)
             swl = (weight - swh.astype(F32)).astype(BF16)
@@ -276,15 +276,15 @@
                 s = softplus(dot(stacked, weights[:, at]) + shift[:, at])
                 du = s * line_ref[line, :, at].astype(F32)
                 for k in range(PIECE):
-                    s_ref[d, g + k] = s[:, cols(k)]
-                    du_ref[d, g + k] = du[:, cols(k)]
+                    s_ref[line, d, g + k] = s[:, cols(k)]
+                    du_ref[line, d, g + k] = du[:, cols(k)]
             enter = dot_nt(pw_ref[which, rank : rank + states, :], u)
             ones = jnp.ones((LANES, LANES), BF16)
             for h in range(length // LANES):
                 for g in range(0, LANES, span):
                     spread = [jnp.where(lane == g + i, enter[:, cols(h)], 0.0) for i in range(span)]
                     at = (h * LANES + g) * states
-                    bb_ref[d, at : at + span * states, :] = dot(jnp.concatenate(spread, axis=0).astype(BF16), ones)
+                    bb_ref[line, d, at : at + span * states, :] = dot(jnp.concatenate(spread, axis=0).astype(BF16), ones)
             return 0
 
         lax.fori_loop(0, 2, prepare, 0)
@@ -294,7 +294,7 @@
             at = pl.ds(pl.multiple_of(i * 32, 32), 32)
             v = line_ref[line, at, :].astype(F32) * skip
             for k in range(groups):
-                acc_ref[k, at, :] = v[:, cols(k)]
+                acc_ref[line, k, at, :] = v[:, cols(k)]
             return 0
 
         lax.fori_loop(0, length // 32, begin, 0)
@@ -302,7 +302,7 @@
     def zeros(per):
         return tuple(tuple((jnp.zeros((8, LANES), F32),) * 2 for _ in range(per)) for _ in range(2))
 
-    def run(per, g0, streams, blocks, init):
+    def run(line, per, g0, streams, blocks, init):
         dec = [
             [[dec_ref[w, g0 + k, 8 * v : 8 * v + 8, :] for v in range(2)] for k in range(per)] for w, _, _, _ in streams
         ]
@@ -314,19 +314,19 @@
         def leave(slot, i, q):
             b = low(i, q)
             states_now = jnp.concatenate([held[slot][q, k] for k in range(per)], axis=1)
-            part = dot(mc_ref[streams[q][1], pl.ds(b, span), :], states_now)
+            part = dot(mc_ref[line, streams[q][1], pl.ds(b, span), :], states_now)
             for k in range(per):
-                acc_ref[g0 + k, pl.ds(b, span), :] += part[:, cols(k)]
+                acc_ref[line, g0 + k, pl.ds(b, span), :] += part[:, cols(k)]
 
         def advance(slot, i, h):
             for j in range(span):
                 for q in range(2):
                     _, d, _, back = streams[q]
                     t = low(i, q) + (j + back * (span - 1 - 2 * j))
-                    enter = [bb_ref[d, pl.ds(pl.multiple_of(t * states + 8 * v, 8), 8), :] for v in range(2)]
+                    enter = [bb_ref[line, d, pl.ds(pl.multiple_of(t * states + 8 * v, 8), 8), :] for v in range(2)]
                     for k in range(per):
-                        s = s_ref[d, g0 + k, pl.ds(t, 8, stride=0), :]
-                        du = du_ref[d, g0 + k, pl.ds(t, 8, stride=0), :]
+                        s = s_ref[line, d, g0 + k, pl.ds(t, 8, stride=0), :]
+                        du = du_ref[line, d, g0 + k, pl.ds(t, 8, stride=0), :]
                         now = [jnp.exp2(s * dec[q][k][v]) * h[q][k][v] + du * enter[v] for v in range(2)]
                         h[q][k] = now
                         held[slot][q, k, j * states : (j + 1) * states, :] = jnp.concatenate(now, axis=0).astype(BF16)
@@ -352,7 +352,7 @@
 
     def settle(line, per, g0):
         for k in range(per):
-            y_ref[line, g0 + k] = acc_ref[g0 + k].astype(BF16)
+            y_ref[line, g0 + k] = acc_ref[line, g0 + k].astype(BF16)
 
     def row_result(c, r, to, which, owner):
         at = pl.ds(c * PER[0], PER[0])
@@ -376,7 +376,7 @@
 
     def outward(c, _):
         per = PER[0]
-        h = run(per, c * per, lines(side), blocks // 2, zeros(per))
+        h = run(0, per, c * per, lines(side), blocks // 2, zeros(per))
         for q in range(2):
             for k in range(per):
                 st_ref[c, q, k] = jnp.concatenate(h[q][k], axis=0).astype(BF16)
@@ -388,7 +388,7 @@
         state_copy(c).wait_recv()
         came = [[sl_ref[c, q, k].astype(F32) for k in range(per)] for q in range(2)]
         init = tuple(tuple((v[:8], v[8:]) for v in part) for part in came)
-        run(per, c * per, lines(1 - side), blocks // 2, init)
+        run(0, per, c * per, lines(1 - side), blocks // 2, init)
         settle(0, per, c * per)
         mates(lambda r, to, which: row_result(c, r, to, which, seat).start())
         for k in range(per):
@@ -398,7 +398,7 @@
 
     def down_and_up(c, _):
         per = PER[1]
-        run(per, c * per, [(2, 0, 0, 0), (3, 1, 0, 1)], blocks, zeros(per))
+        run(1, per, c * per, [(2, 0, 0, 0), (3, 1, 0, 1)], blocks, zeros(per))
         settle(1, per, c * per)
         others(lambda step, peer: column_result(c, step, peer, row).start())
         for k in range(per):
@@ -408,10 +408,10 @@
     mates(lambda r, to, which: row_tokens(r, to, which, to).wait_recv())
     ready(0)
     lax.fori_loop(0, groups // PER[0], outward, 0)
-    lax.fori_loop(0, groups // PER[0], inward, 0)
     others(lambda step, peer: column_tokens(step, peer, peer).wait_recv())
     ready(1)
     lax.fori_loop(0, groups // PER[1], down_and_up, 0)
+    lax.fori_loop(0, groups // PER[0], inward, 0)
     mates(lambda r, to, which: row_tokens(r, to, which, seat).wait_send())
     others(lambda step, peer: column_tokens(step, peer, row).wait_send())
     for c in range(groups // PER[0]):
@@ -480,14 +480,14 @@
             pltpu.VMEM((groups, tokens, LANES), F32),
             pltpu.VMEM((2, length, width), BF16),
             pltpu.VMEM((tokens, width), F32),
-            pltpu.VMEM((2, groups, length, LANES), F32),
-            pltpu.VMEM((2, groups, length, LANES), F32),
-            pltpu.VMEM((2, length * states, LANES), F32),
-            pltpu.VMEM((2, length, span * states), BF16),
+            pltpu.VMEM((2, 2, groups, length, LANES), F32),
+            pltpu.VMEM((2, 2, groups, length, LANES), F32),
+            pltpu.VMEM((2, 2, length * states, LANES), F32),
+            pltpu.VMEM((2, 2, length, span * states), BF16),
             pltpu.VMEM((dl.shape[0], groups, states, LANES), F32),
             pltpu.VMEM((2, per, span * states, LANES), BF16),
             pltpu.VMEM((2, per, span * states, LANES), BF16),
-            pltpu.VMEM((groups, length, LANES), F32),
+            pltpu.VMEM((2, groups, length, LANES), F32),
             pltpu.VMEM((2, groups, length, LANES), BF16),
             pltpu.VMEM((2, groups, n, tc, LANES), BF16),
             pltpu.VMEM((groups, tokens, LANES), F32),

time: 65.9 us -> 61.2 us (0.929)
  Pallas kernels: 64.2 us -> 59.5 us
    pallas_call x1, Pallas kernels: 64.2 us -> 59.5 us  [local(): pl.pallas_call(functools.partial(block_kernel, n), out_shape=jax.ShapeDty...]
where the time goes in v4:
time: 61.2 us; the launch traced here: 61.1 us
  Pallas kernels  59.5 us (97%)
  local copies, waits for them, and re-layouts  1.62 us (3%)
    pallas_call x1, Pallas kernels, local(): pl.pallas_call(functools.partial(block_kernel, n), out_shape=jax.ShapeDty...  59.5 us
    unnamed x1, local copies, waits for them, and re-layouts  1.62 us

profile of v4, /device:TPU:1, one launch (start us, length us, event | category | flops | bytes accessed | tf_op | source)
XLA Modules:
  0.0 61.1 jit_solution(15912223017663410574)
XLA Ops:
  0.0 59.5 %shard_map.118 = bf16[16,16,384]{2,1,0:T(8,128)(2,1)} custom-call(bf16[16,16,384]{2,1,0:T(8,128)(2,1)} %x_hbm.1, f32[384]{0:T(512)} %gain_hbm.1, bf16[384,1536]{1,0:T(8,128)(2,1)} %wi_hbm.1, f32[3,3,768]{2,1,0:T(4,128)} %cw_hbm.1, f32[768]{0:T(1024)} %cb_hbm.1, bf16[4,56,768]{2,1,0:T(8,128)(2,1)} %bitcast.2, f32[4,24,768]{2,1,0:T(8,128)} %sw_hbm.1, ...), custom_call_target="tpu_custom_call" | custom-call | tf_op jit(solution)/shard_map/pallas_call | solution.py:467
  59.5 1.6 %copy.14 = bf16[16,16,384]{2,1,0:T(8,128)(2,1)} copy(bf16[16,16,384]{2,1,0:T(8,128)(2,1)} %shard_map.118) | data formatting | bytes 393216

commit v5 on v4

--- a/solution.py
+++ b/solution.py
@@ -95,9 +95,10 @@
     there = (x_hbm, gain_hbm, wi_hbm, cw_hbm, cb_hbm, pw_hbm, sw_hbm, sb_hbm, dl_hbm, sk_hbm, og_hbm, wo_hbm)
     here = (x_ref, gain_ref, wi_ref, cw_ref, cb_ref, pw_ref, sw_ref, sb_ref, dl_ref, sk_ref, og_ref, wo_ref)
     fetch = [pltpu.make_async_copy(src, dst, own_sem.at[i]) for i, (src, dst) in enumerate(zip(there, here))]
-    for copy in fetch:
+    fetch[0].start()
+    greeted = greet(n, n)
+    for copy in fetch[1:]:
         copy.start()
-    greeted = greet(n, n)
 
     half = n // 2
     side, seat = col // half, lax.rem(col, half)
@@ -134,7 +135,8 @@
             nf_ref[k, at, :] = v[:, cols(k)]
         return 0
 
-    lax.fori_loop(0, tokens // step, norm, 0)
+    hb_ref[...] = jnp.zeros_like(hb_ref)
+    lax.fori_loop(0, tokens // step, norm, 0, unroll=2)
     for k in range(channels // LANES):
         strip_ref[0, :, cols(k)] = nf_ref[k, pl.ds(0, tr, stride=tc), :].astype(BF16)
         strip_ref[1, :, cols(k)] = nf_ref[k, pl.ds(tc - 1, tr, stride=tc), :].astype(BF16)
@@ -162,7 +164,7 @@
             pad_ref[k, pl.ds(1 + i * 4, 4), 8 : 8 + tc, :] = inner[:, cols(k)].reshape(4, tc, LANES)
         return 0
 
-    lax.fori_loop(0, tokens // step, project, 0)
+    lax.fori_loop(0, tokens // step, project, 0, unroll=2)
     for copy in halos:
         copy.wait()
     edge = dot(halo_ref[...], wi_ref[:, :width]).astype(BF16).astype(F32)
@@ -216,14 +218,14 @@
 
         return 0
 
-    lax.fori_loop(2, n + 2, convolve, 0)
+    lax.fori_loop(2, n + 2, convolve, 0, unroll=2)
 
     def flip(j, _):
         for k in range(groups):
             actt_ref[j, :, cols(k)] = actf_ref[k, pl.ds(j, tr, stride=tc), :].astype(BF16)
         return 0
 
-    lax.fori_loop(0, tc, flip, 0)
+    lax.fori_loop(0, tc, flip, 0, unroll=4)
     others(lambda step, peer: column_tokens(step, peer, row).start())
     for which in range(2):
         line_ref[0, tile(which * half + seat), :] = act_ref[2 * seat + which]
@@ -235,7 +237,7 @@
         gate_ref[at, :] = silu(gate)
         return 0
 
-    lax.fori_loop(0, tokens // step, gates, 0)
+    lax.fori_loop(0, tokens // step, gates, 0, unroll=2)
     for i in range(5, len(fetch)):
         fetch[i].wait()
 
@@ -297,7 +299,7 @@
                 acc_ref[line, k, at, :] = v[:, cols(k)]
             return 0
 
-        lax.fori_loop(0, length // 32, begin, 0)
+        lax.fori_loop(0, length // 32, begin, 0, unroll=2)
 
     def zeros(per):
         return tuple(tuple((jnp.zeros((8, LANES), F32),) * 2 for _ in range(per)) for _ in range(2))
@@ -311,12 +313,14 @@
             _, _, first, back = streams[q]
             return pl.multiple_of(first + (i + back * (blocks - 1 - 2 * i)) * span, span)
 
-        def leave(slot, i, q):
+        def leave(slot, i, q, spare=None):
             b = low(i, q)
+            to = b if spare is None else jnp.where(spare, length, b)
+            to = pl.multiple_of(to, span)
             states_now = jnp.concatenate([held[slot][q, k] for k in range(per)], axis=1)
             part = dot(mc_ref[line, streams[q][1], pl.ds(b, span), :], states_now)
             for k in range(per):
-                acc_ref[line, g0 + k, pl.ds(b, span), :] += part[:, cols(k)]
+                acc_ref[line, g0 + k, pl.ds(to, span), :] += part[:, cols(k)]
 
         def advance(slot, i, h):
             for j in range(span):
@@ -335,16 +339,13 @@
         def body(i, h):
             h = [[list(v) for v in part] for part in h]
             for q in range(2):
-                leave(1, jnp.maximum(2 * i - 1, 0), q)
+                leave(1, jnp.maximum(2 * i - 1, 0), q, i == 0)
             h = advance(0, 2 * i, h)
             for q in range(2):
                 leave(0, 2 * i, q)
             h = advance(1, 2 * i + 1, h)
             return tuple(tuple(tuple(v) for v in part) for part in h)
 
-        for q in range(2):
-            for k in range(per):
-                hb_ref[q, k] = jnp.zeros_like(hb_ref[q, k])
         h = lax.fori_loop(0, blocks // 2, body, init)
         for q in range(2):
             leave(1, blocks - 1, q)
@@ -352,7 +353,7 @@
 
     def settle(line, per, g0):
         for k in range(per):
-            y_ref[line, g0 + k] = acc_ref[line, g0 + k].astype(BF16)
+            y_ref[line, g0 + k] = acc_ref[line, g0 + k, :length].astype(BF16)
 
     def row_result(c, r, to, which, owner):
         at = pl.ds(c * PER[0], PER[0])
@@ -412,11 +413,6 @@
     ready(1)
     lax.fori_loop(0, groups // PER[1], down_and_up, 0)
     lax.fori_loop(0, groups // PER[0], inward, 0)
-    mates(lambda r, to, which: row_tokens(r, to, which, seat).wait_send())
-    others(lambda step, peer: column_tokens(step, peer, row).wait_send())
-    for c in range(groups // PER[0]):
-        state_copy(c).wait_send()
-        mates(lambda r, to, which: row_result(c, r, to, which, to).wait_recv())
     for c in range(groups // PER[1]):
         others(lambda step, peer: column_result(c, step, peer, peer).wait_recv())
 
@@ -425,7 +421,10 @@
                 cf_ref[k, tile(j), :] = land_ref[1, k, j].astype(F32)
             return 0
 
-        lax.fori_loop(0, tc, widen, 0)
+        lax.fori_loop(0, tc, widen, 0, unroll=4)
+
+    for c in range(groups // PER[0]):
+        mates(lambda r, to, which: row_result(c, r, to, which, to).wait_recv())
 
     def finish(r, _):
         other = jnp.concatenate([cf_ref[k, pl.ds(r, tc, stride=tr), :] for k in range(groups)], axis=1)
@@ -435,10 +434,13 @@
         go_ref[tile(r), :] = (v * gate_ref[tile(r), :]).astype(BF16)
         return 0
 
-    lax.fori_loop(0, tr, finish, 0)
+    lax.fori_loop(0, tr, finish, 0, unroll=8)
     out_ref[...] = dot(go_ref[...], wo_ref[...]).astype(BF16).reshape(out_ref.shape)
 
+    mates(lambda r, to, which: row_tokens(r, to, which, seat).wait_send())
+    others(lambda step, peer: column_tokens(step, peer, row).wait_send())
     for c in range(groups // PER[0]):
+        state_copy(c).wait_send()
         mates(lambda r, to, which: row_result(c, r, to, which, seat).wait_send())
     for c in range(groups // PER[1]):
         others(lambda step, peer: column_result(c, step, peer, row).wait_send())
@@ -487,7 +489,7 @@
             pltpu.VMEM((dl.shape[0], groups, states, LANES), F32),
             pltpu.VMEM((2, per, span * states, LANES), BF16),
             pltpu.VMEM((2, per, span * states, LANES), BF16),
-            pltpu.VMEM((2, groups, length, LANES), F32),
+            pltpu.VMEM((2, groups, length + span, LANES), F32),
             pltpu.VMEM((2, groups, length, LANES), BF16),
             pltpu.VMEM((2, groups, n, tc, LANES), BF16),
             pltpu.VMEM((groups, tokens, LANES), F32),

time: 61.2 us -> 58.1 us (0.949)
  Pallas kernels: 59.5 us -> 56.3 us
    pallas_call x1, Pallas kernels: 59.5 us -> 56.3 us  [local(): pl.pallas_call(functools.partial(block_kernel, n), out_shape=jax.ShapeDty...]
where the time goes in v5:
time: 58.1 us; the launch traced here: 58 us
  Pallas kernels  56.3 us (97%)
  local copies, waits for them, and re-layouts  1.62 us (3%)
    pallas_call x1, Pallas kernels, local(): pl.pallas_call(functools.partial(block_kernel, n), out_shape=jax.ShapeDty...  56.3 us
    unnamed x1, local copies, waits for them, and re-layouts  1.62 us

profile of v5, /device:TPU:1, one launch (start us, length us, event | category | flops | bytes accessed | tf_op | source)
XLA Modules:
  0.0 58.0 jit_solution(7760006324681274499)
XLA Ops:
  0.0 56.3 %shard_map.118 = bf16[16,16,384]{2,1,0:T(8,128)(2,1)} custom-call(bf16[16,16,384]{2,1,0:T(8,128)(2,1)} %x_hbm.1, f32[384]{0:T(512)} %gain_hbm.1, bf16[384,1536]{1,0:T(8,128)(2,1)} %wi_hbm.1, f32[3,3,768]{2,1,0:T(4,128)} %cw_hbm.1, f32[768]{0:T(1024)} %cb_hbm.1, bf16[4,56,768]{2,1,0:T(8,128)(2,1)} %bitcast.2, f32[4,24,768]{2,1,0:T(8,128)} %sw_hbm.1, ...), custom_call_target="tpu_custom_call" | custom-call | tf_op jit(solution)/shard_map/pallas_call | solution.py:469
  56.3 1.6 %copy.14 = bf16[16,16,384]{2,1,0:T(8,128)(2,1)} copy(bf16[16,16,384]{2,1,0:T(8,128)(2,1)} %shard_map.118) | data formatting | bytes 393216

commit v6 on v5

--- a/solution.py
+++ b/solution.py
@@ -136,7 +136,7 @@
         return 0
 
     hb_ref[...] = jnp.zeros_like(hb_ref)
-    lax.fori_loop(0, tokens // step, norm, 0, unroll=2)
+    lax.fori_loop(0, tokens // step, norm, 0, unroll=4)
     for k in range(channels // LANES):
         strip_ref[0, :, cols(k)] = nf_ref[k, pl.ds(0, tr, stride=tc), :].astype(BF16)
         strip_ref[1, :, cols(k)] = nf_ref[k, pl.ds(tc - 1, tr, stride=tc), :].astype(BF16)
@@ -218,7 +218,7 @@
 
         return 0
 
-    lax.fori_loop(2, n + 2, convolve, 0, unroll=2)
+    lax.fori_loop(2, n + 2, convolve, 0, unroll=4)
 
     def flip(j, _):
         for k in range(groups):
@@ -246,7 +246,7 @@
             dec_ref[d, k] = jnp.exp(dl_ref[d, :, cols(k)]) * -LOG2E
         return 0
 
-    lax.fori_loop(0, dl_ref.shape[0], rates, 0)
+    lax.fori_loop(0, dl_ref.shape[0], rates, 0, unroll=2)
 
     span = 16
     blocks = length // span
@@ -289,7 +289,7 @@
                     bb_ref[line, d, at : at + span * states, :] = dot(jnp.concatenate(spread, axis=0).astype(BF16), ones)
             return 0
 
-        lax.fori_loop(0, 2, prepare, 0)
+        lax.fori_loop(0, 2, prepare, 0, unroll=2)
         skip = sk_ref[pl.ds(line * 2, 1), :] + sk_ref[pl.ds(line * 2 + 1, 1), :]
 
         def begin(i, _):
@@ -434,7 +434,7 @@
         go_ref[tile(r), :] = (v * gate_ref[tile(r), :]).astype(BF16)
         return 0
 
-    lax.fori_loop(0, tr, finish, 0, unroll=8)
+    lax.fori_loop(0, tr, finish, 0, unroll=16)
     out_ref[...] = dot(go_ref[...], wo_ref[...]).astype(BF16).reshape(out_ref.shape)
 
     mates(lambda r, to, which: row_tokens(r, to, which, seat).wait_send())

time: 58.1 us -> 57.4 us (0.988)
  Pallas kernels: 56.3 us -> 55.7 us
    pallas_call x1, Pallas kernels: 56.3 us -> 55.7 us  [local(): pl.pallas_call(functools.partial(block_kernel, n), out_shape=jax.ShapeDty...]
where the time goes in v6:
time: 57.4 us; the launch traced here: 57.3 us
  Pallas kernels  55.7 us (97%)
  local copies, waits for them, and re-layouts  1.62 us (3%)
    pallas_call x1, Pallas kernels, local(): pl.pallas_call(functools.partial(block_kernel, n), out_shape=jax.ShapeDty...  55.7 us
    unnamed x1, local copies, waits for them, and re-layouts  1.62 us

profile of v6, /device:TPU:1, one launch (start us, length us, event | category | flops | bytes accessed | tf_op | source)
XLA Modules:
  0.0 57.3 jit_solution(4704765330107631208)
XLA Ops:
  0.0 55.7 %shard_map.118 = bf16[16,16,384]{2,1,0:T(8,128)(2,1)} custom-call(bf16[16,16,384]{2,1,0:T(8,128)(2,1)} %x_hbm.1, f32[384]{0:T(512)} %gain_hbm.1, bf16[384,1536]{1,0:T(8,128)(2,1)} %wi_hbm.1, f32[3,3,768]{2,1,0:T(4,128)} %cw_hbm.1, f32[768]{0:T(1024)} %cb_hbm.1, bf16[4,56,768]{2,1,0:T(8,128)(2,1)} %bitcast.2, f32[4,24,768]{2,1,0:T(8,128)} %sw_hbm.1, ...), custom_call_target="tpu_custom_call" | custom-call | tf_op jit(solution)/shard_map/pallas_call | solution.py:469
  55.7 1.6 %copy.14 = bf16[16,16,384]{2,1,0:T(8,128)(2,1)} copy(bf16[16,16,384]{2,1,0:T(8,128)(2,1)} %shard_map.118) | data formatting | bytes 393216
